TPU v7x, 256 devices: a whole 4x4x8 slice. The times are simulated.
256 devices in a mesh: stripe: 8 (over y, x_hi), scan: 32 (over z, x_lo, core).
Axes of the slice: x: 4 (x_hi: 2, x_lo: 2; x = x_hi * 2 + x_lo), y: 4, z: 8, core: 2. Of those that a mesh axis runs over, the one named last changes fastest.
Arguments:
- dose: bfloat16 [1600, 3200], P('stripe', 'scan'), may hold values from 0 to 4
- target: int32 [1600, 3200], P('stripe', 'scan'), may hold values 0 or 1
- psf: bfloat16 [61, 61], replicated, may hold values from 0 to 0.025
Outputs:
- resist: float32 [1600, 3200], P('stripe', 'scan')
- dose_out: float32 [1600, 3200], P('stripe', 'scan')
All inputs are finite; a program needn't handle non-finite values. No bound on the sum of `target` on one device may be relied on, other than what follows from the above.
Results may differ from a plain program's by a relative error of at most 0.0003.
Values may be sent and summed in bfloat16 or wider, within the bound.
A program may use at most 64 MiB of HBM per device.

v0:
```python
import math

import jax
import jax.numpy as jnp
from jax import lax
from jax.experimental import pallas as pl
from jax.experimental.pallas import tpu as pltpu
from jax.sharding import PartitionSpec as P

TX, TY = 200, 100
TAPS = 61
COARSE = 25
SIGMA = 40
ITERS = 4
RIM = 30
BACK = 0.6
GAIN = 3.0
LEVEL = 1.5
STEP = 0.5
CROW, CCOL = TX // COARSE, TY // COARSE
ADJ_SCALE = BACK / (COARSE * COARSE)

MESH = pl.DeviceIdType.MESH
F32, BF16 = jnp.float32, jnp.bfloat16
HI = lax.Precision.HIGHEST

EROWS = 336
CROWS = 272
AOUT = 264
AIN = 320
BIN = 256
PHASES = ITERS + 1
SIDE = 208
EDGE = 64
HALO = 2 * SIDE + 6 * EDGE


def iota(shape, dim):
    return lax.broadcasted_iota(jnp.int32, shape, dim)


def dot(a, b, precision=None):
    return jnp.dot(a, b, precision=precision, preferred_element_type=F32)


def dot_nt(a, b, precision=None):
    return lax.dot_general(
        a, b, (((1,), (1,)), ((), ())), precision=precision, preferred_element_type=F32
    )


def gauss(dist):
    d = dist.astype(F32)
    return jnp.exp(-d * d / (2.0 * SIGMA * SIGMA)) / (math.sqrt(2.0 * math.pi) * SIGMA)


def cell_of(col):
    out = jnp.full(col.shape, -3, jnp.int32)
    for k in range(-2, 7):
        out = out + jnp.where(col >= COARSE * k, 1, 0)
    return out


def kernel(
    ns, nn, dose_ref, target_ref, psf_ref, resist_ref, updated_ref,
    g1, g2, halo, tile, bottom, et0, et1, ct0, ct1, at0, at1, wa, wf, vv,
    ps, rf, ra, fr, xa, xb, err, own, zs, sc, m1, cu, ub0, ub1, bk,
    send_sem, recv_sem,
):
    s = lax.axis_index("stripe")
    n = lax.axis_index("scan")
    ncx, ncy = ns * CROW, nn * CCOL
    up, down = lax.rem(s + ns - 1, ns), lax.rem(s + 1, ns)
    left, right = lax.rem(n + nn - 1, nn), lax.rem(n + 1, nn)

    barrier = pltpu.get_barrier_semaphore()

    def hello(a, b):
        pl.semaphore_signal(barrier, inc=1, device_id=(a, b), device_id_type=MESH)

    for k in range(1, ns):
        hello(lax.rem(s + k, ns), n)
    for k in range(1, nn):
        hello(s, lax.rem(n + k, nn))
    for a in (up, down):
        for b in (left, right):
            hello(a, b)

    lane = iota((1, 128), 1)

    def field_out(value):
        tile[0:TX, :] = value.astype(BF16)
        bottom[...] = value[TX - EDGE:, :].astype(BF16)

    def col_sum(ref):
        total = ref[pl.ds(0, CROW, stride=COARSE), :]
        for u in range(1, COARSE):
            total = total + ref[pl.ds(u, CROW, stride=COARSE), :]
        return total

    pick = jnp.where(cell_of(iota((16, 128), 1)) == iota((16, 128), 0), 1.0, 0.0)
    pick = jnp.where((iota((16, 128), 0) < CCOL) & (iota((16, 128), 1) < TY), pick, 0.0)
    pick2 = jnp.where(cell_of(iota((16, 128), 1)) == iota((16, 128), 0) - 10, 1.0, 0.0)
    pick2 = jnp.where(
        (iota((16, 128), 0) >= 8) & (iota((16, 128), 1) < TY)
        & (iota((16, 128), 0) < 10 + CCOL) & (iota((16, 128), 0) >= 10), pick2, 0.0)
    picks = pick + pick2

    zs[...] = jnp.zeros_like(zs)
    sc[...] = jnp.zeros_like(sc)

    def payload(err_cols, cur_cols, spread):
        both = dot_nt(picks, jnp.concatenate([err_cols, cur_cols], axis=0), HI)
        sc[:, 0:16] = both
        first = jnp.where(lane < CROW, sc[0:8, :], 0.0)
        second = jnp.where((lane >= 8) & (lane < 16), sc[8:16, :], 0.0)
        sums = pltpu.roll(first, s * CROW, 1)
        cells = pltpu.roll(second, 64 - 8 + s * CROW, 1) * (1.0 / (COARSE * COARSE))
        if spread is not None:
            zs[:, 0:8] = spread
            part = jnp.zeros((8, 128), F32)
            for d in range(5):
                part = part + pltpu.roll(zs[8 * d:8 * d + 8, :], 62 + d + s * CROW, 1)
            cells = cells - (STEP / (COARSE * COARSE)) * part
        return jnp.where(lane < 64, sums, cells)

    def start_global1(t, value):
        g1[t, s] = value
        for k in range(1, ns):
            pltpu.make_async_remote_copy(
                g1.at[t, s], g1.at[t, s], send_sem.at[0], recv_sem.at[t, 0],
                device_id=(lax.rem(s + k, ns), n), device_id_type=MESH,
            ).start()

    def start_global2(t, value):
        g2[t, n] = value
        for k in range(1, nn):
            pltpu.make_async_remote_copy(
                g2.at[t, n], g2.at[t, n], send_sem.at[1], recv_sem.at[t, 1],
                device_id=(s, lax.rem(n + k, nn)), device_id_type=MESH,
            ).start()

    def start_halo(t):
        def go(src, first, rows, a, b):
            pltpu.make_async_remote_copy(
                src, halo.at[t, pl.ds(first, rows)], send_sem.at[2], recv_sem.at[t, 2],
                device_id=(a, b), device_id_type=MESH,
            ).start()

        top = tile.at[pl.ds(0, EDGE)]
        first = 2 * SIDE
        go(tile, 0, SIDE, s, right)
        go(tile, SIDE, SIDE, s, left)
        go(bottom, first, EDGE, down, n)
        go(top, first + EDGE, EDGE, up, n)
        go(bottom, first + 2 * EDGE, EDGE, down, right)
        go(bottom, first + 3 * EDGE, EDGE, down, left)
        go(top, first + 4 * EDGE, EDGE, up, right)
        go(top, first + 5 * EDGE, EDGE, up, left)

    def all_of(ref, sem_send, sem_recv):
        return pltpu.make_async_remote_copy(
            ref, ref, sem_send, sem_recv, device_id=(s, right), device_id_type=MESH
        )

    def of_global1(t):
        return all_of(g1.at[t, pl.ds(0, ns - 1)], send_sem.at[0], recv_sem.at[t, 0])

    def of_global2(t):
        return all_of(g2.at[t, pl.ds(0, nn - 1)], send_sem.at[1], recv_sem.at[t, 1])

    def of_halo(t):
        return all_of(halo.at[t], send_sem.at[2], recv_sem.at[t, 2])

    def assemble(t, centre):
        yes = lambda c: jnp.where(c, 1.0, 0.0).astype(F32)
        has_up, has_down = yes(s > 0), yes(s < ns - 1)
        has_left, has_right = yes(n > 0), yes(n < nn - 1)
        first = 2 * SIDE

        def band(row, rows, mid, lhs, rhs, flag):
            lhs = pltpu.roll(lhs, 28, 1) * (has_left * flag)
            rhs = pltpu.roll(rhs, TY, 1) * (has_right * flag)
            et0[row:row + rows, :] = jnp.where(lane < TY, mid * flag, rhs)
            et1[row:row + rows, :] = jnp.where(lane < 32, rhs, jnp.where(lane >= 68, lhs, 0.0))

        def part(k, rows):
            return halo[t, pl.ds(k, rows), :].astype(F32)

        band(0, EDGE, part(first, EDGE), part(first + 2 * EDGE, EDGE), part(first + 3 * EDGE, EDGE), has_up)
        band(EDGE, TX, centre, part(0, TX), part(SIDE, TX), jnp.float32(1.0))
        band(EDGE + TX, EDGE, part(first + EDGE, EDGE), part(first + 4 * EDGE, EDGE), part(first + 5 * EDGE, EDGE), has_down)

    def global1_result(t):
        total = g1[t, 0]
        for k in range(1, ns):
            total = total + g1[t, k]
        return dot(total, m1[...], HI)

    def global2_result(t):
        stack = g2[t].reshape(nn * 8, 128)
        turned = jnp.transpose(stack)[0:32, :]
        return dot(turned, cu[...], HI)

    def set_back(out):
        value = BACK * (out[16:24, 256:384] + out[24:32, 384:512])
        for u in range(COARSE):
            bk[pl.ds(u, CROW, stride=COARSE), :] = value

    ps[...] = jnp.zeros_like(ps)
    ps[0:TAPS, 0:TAPS] = psf_ref[...].astype(F32)
    taps = ps[...]
    taps_h = taps.astype(BF16)
    b_at, l_at = iota((128, 128), 0), iota((128, 128), 1)
    perm_f = jnp.where((l_at == lax.rem(RIM - b_at + 256, 128)) & (b_at < TAPS), 1.0, 0.0).astype(BF16)
    perm_a = jnp.where((l_at == lax.rem(b_at - RIM + 256, 128)) & (b_at < TAPS), 1.0, 0.0).astype(BF16)
    flip = jnp.where(iota((64, 64), 1) == TAPS - 1 - iota((64, 64), 0), 1.0, 0.0).astype(BF16)
    rf[...] = dot(taps_h, perm_f)
    ra[...] = dot(dot(flip, taps_h).astype(BF16), perm_a)

    dose = jnp.zeros((TX, 128), F32)
    own[...] = dose
    own[:, 0:TY] = dose_ref[...].astype(F32)
    tile[...] = jnp.zeros_like(tile)
    field_out(own[...])
    first_payload = payload(jnp.zeros((8, 128), F32), col_sum(own), None)

    g_row = jnp.bitwise_and(b_at, 63)
    full_rows = gauss(iota((ncx, ncx), 0) - iota((ncx, ncx), 1))
    twice = dot(full_rows, gauss(iota((ncx, 128), 0) - (s * CROW + iota((ncx, 128), 1) - 16)), HI)
    upper = jnp.concatenate([twice, jnp.zeros((128 - ncx, 128), F32)], axis=0)
    low = b_at < 64
    table = jnp.where(low & (l_at < 12), gauss(g_row - (s * CROW + l_at - 2)), 0.0)
    table = table + jnp.where(low & (l_at >= 16) & (l_at < 24), upper, 0.0)
    table = table + jnp.where((~low) & (l_at >= 24) & (l_at < 32), gauss(g_row - (s * CROW + l_at - 24)), 0.0)
    table = jnp.where(g_row < ncx, table, 0.0)
    m1[...] = table

    pl.semaphore_wait(barrier, ns - 1 + nn - 1 + 4)
    start_global1(0, first_payload)
    start_halo(0)

    rows8 = nn * 8
    q = jnp.bitwise_and(iota((rows8, 256), 0), 7)
    dev = iota((rows8, 256), 0) // 8
    pos = iota((rows8, 256), 1)
    col = jnp.where(pos < 160, pos, pos - 256)
    cu[:, 0:256] = jnp.where(q < CCOL, gauss(CCOL * dev + q - (CCOL * n + cell_of(col))), 0.0)
    q1, dev1 = q[:, 0:128], dev[:, 0:128]
    lane_cell = CCOL * n + cell_of(iota((rows8, 128), 1))
    mid_at = iota((ncy, 128), 0)
    mid = gauss(mid_at - (CCOL * n + cell_of(iota((ncy, 128), 1))))
    qf = jnp.bitwise_and(iota((rows8, ncy), 0), 7)
    outer = jnp.where(qf < CCOL, gauss(CCOL * (iota((rows8, ncy), 0) // 8) + qf - iota((rows8, ncy), 1)), 0.0)
    cu[:, 256:384] = (-STEP * ADJ_SCALE) * dot(outer, mid, HI)
    at = CCOL * dev1 + q1 - 2
    cu[:, 384:512] = jnp.where((at >= 0) & (at < ncy), gauss(at - lane_cell), 0.0)

    near = jnp.abs(b_at - l_at) <= RIM

    def circulant(row):
        full = pltpu.roll(jnp.broadcast_to(row, (128, 128)), 0, 1, stride=1, stride_axis=0)
        return jnp.where(near, full, 0.0).astype(BF16), jnp.where(near, 0.0, full).astype(BF16)

    def one_pair(k, carry):
        pair, shift = k // 8, lax.rem(k, 8)
        at_row = pl.multiple_of(shift * 256, 256)
        for half in range(2):
            tap = pair * 16 + half * 8 + shift
            same, other = circulant(rf[pl.ds(tap, 1), :])
            wf[pair, pl.ds(at_row, 128), half * 128:half * 128 + 128] = same
            wf[pair, pl.ds(at_row + 128, 128), half * 128:half * 128 + 128] = other
            same, other = circulant(ra[pl.ds(tap, 1), :])
            group = pair * 2 + half
            wa[group, pl.ds(at_row, 128), 0:128] = same
            wa[group, pl.ds(at_row, 128), 128:256] = other
            wa[group, pl.ds(at_row + 128, 128), 0:128] = other
            wa[group, pl.ds(at_row + 128, 128), 128:256] = same
        return carry

    lax.fori_loop(0, 32, one_pair, 0)

    of_global1(0).wait_recv()
    start_global2(0, global1_result(0))

    k_at, a_at = iota((128, 64), 0), iota((128, 64), 1)
    u_at = k_at // 5
    low_a = COARSE * (k_at - 5 * u_at - 2) - u_at + RIM
    rows_w = jnp.where((a_at >= low_a) & (a_at < low_a + COARSE), 1.0, 0.0).astype(BF16)
    x_at = -2 * COARSE - jnp.where(l_at < 16, l_at, l_at - 128)
    cols_w = jnp.where((b_at >= x_at + RIM) & (b_at < x_at + RIM + COARSE), 1.0, 0.0)
    fr[...] = dot(dot(rows_w, taps_h), cols_w, HI)
    j8 = iota((8, 128), 0)
    c8 = iota((8, 128), 1)
    xx = COARSE * (j8 - 2) - c8
    inside = (xx >= RIM - 84) & (xx <= RIM) & (c8 < TY)
    for u in range(COARSE):
        pieces = []
        for d in range(5):
            row = jnp.broadcast_to(fr[5 * u + d:5 * u + d + 1, :], (8, 128))
            row = pltpu.roll(pltpu.roll(row, 0, 1, stride=12, stride_axis=0), 0, 1, stride=13, stride_axis=0)
            pieces.append(jnp.where(inside, row, 0.0))
        pieces.append(jnp.zeros((8, 128), F32))
        block = jnp.concatenate(pieces, axis=0)
        for split in range(3):
            rounded = block.astype(BF16)
            vv[48 * split:48 * split + 48, 128 * u:128 * u + 128] = rounded
            block = block - rounded.astype(F32)

    et0[AIN + 8:, :] = jnp.zeros((EROWS - AIN - 8, 128), F32)
    et1[AIN + 8:, :] = jnp.zeros((EROWS - AIN - 8, 128), F32)
    ct0[AOUT:, :] = jnp.zeros((CROWS - AOUT, 128), F32)
    ct1[AOUT:, :] = jnp.zeros((CROWS - AOUT, 128), F32)

    of_halo(0).wait_recv()
    assemble(0, own[...])
    ct0[0:AOUT, :] = et0[32:32 + AOUT, :]
    ct1[0:AOUT, :] = et1[32:32 + AOUT, :]

    of_global2(0).wait_recv()
    set_back(global2_result(0))
    of_global1(0).wait_send()
    of_global2(0).wait_send()
    of_halo(0).wait_send()

    yes = lambda c: jnp.where(c, 1.0, 0.0).astype(F32)
    row_ok = jnp.ones((AOUT, 1), F32)
    r_at = iota((AOUT, 1), 0) - 32
    row_ok = jnp.where(r_at < 0, yes(s > 0), jnp.where(r_at >= TX, yes(s < ns - 1), 1.0))
    mask0 = jnp.where(lane < TY, 1.0, yes(n < nn - 1))
    mask1 = jnp.where(lane < 32, yes(n < nn - 1), yes(n > 0))

    def iteration(t, carry):
        for k in range(8):
            xb[:, 256 * k:256 * k + 128] = ct0[k + 2:k + 2 + BIN, :].astype(BF16)
            xb[:, 256 * k + 128:256 * k + 256] = ct1[k + 2:k + 2 + BIN, :].astype(BF16)
        blurred = None
        for pair in range(4):
            piece = dot(xb[...], wf[pair])
            lo = 16 * pair
            both = piece[lo:lo + TX, 0:128] + piece[lo + 8:lo + 8 + TX, 128:256]
            blurred = both if blurred is None else blurred + both
        exposure = blurred + bk[...]
        resist = jax.nn.sigmoid(GAIN * (exposure - LEVEL))
        own[:, 0:TY] = target_ref[...].astype(F32)
        error = (resist - own[...]) * GAIN * resist * (1.0 - resist)
        error = jnp.where(lane < TY, error, 0.0)
        err[...] = error
        half = error.astype(BF16).astype(F32)
        own[...] = half
        field_out(half)
        resist_ref[...] = resist[:, 0:TY]

        cells_in = jnp.concatenate(
            [own[pl.ds(u, CROW, stride=COARSE), :].astype(BF16) for u in range(COARSE)], axis=1)
        three = dot_nt(vv[...], cells_in)
        spread = three[0:40] + three[48:88] + three[96:136]
        cur_cols = jnp.where(lane < TY, col_sum(ct0.at[pl.ds(32, TX)]), 0.0)
        start_global1(t, payload(col_sum(err), cur_cols, spread))
        start_halo(t)

        of_global1(t).wait_recv()
        start_global2(t, global1_result(t))

        of_halo(t).wait_recv()
        assemble(t, own[...])
        for k in range(8):
            xa[:, 256 * k:256 * k + 128] = et0[k + 2:k + 2 + AIN, :].astype(BF16)
            xa[:, 256 * k + 128:256 * k + 256] = et1[k + 2:k + 2 + AIN, :].astype(BF16)
        for group in range(8):
            piece = dot(xa[...], wa[group])
            lo = 8 * group
            if group == 0:
                at0[...] = piece[lo:lo + AOUT, 0:128]
                at1[...] = piece[lo:lo + AOUT, 128:256]
            else:
                at0[...] += piece[lo:lo + AOUT, 0:128]
                at1[...] += piece[lo:lo + AOUT, 128:256]

        of_global2(t).wait_recv()
        out = global2_result(t)
        for u in range(COARSE):
            for ref, first in ((ub0, 0), (ub1, 128)):
                ref[pl.ds(6 + u, 8, stride=COARSE), :] = out[0:8, first:first + 128]
                ref[pl.ds(206 + u, 8, stride=COARSE), :] = out[8:16, first:first + 128]
        set_back(out)
        new0 = ct0[0:AOUT, :] - STEP * (at0[...] + ADJ_SCALE * ub0[24:24 + AOUT, :])
        new1 = ct1[0:AOUT, :] - STEP * (at1[...] + ADJ_SCALE * ub1[24:24 + AOUT, :])
        updated_ref[...] = new0[32:32 + TX, 0:TY]
        ct0[0:AOUT, :] = new0.astype(BF16).astype(F32) * (row_ok * mask0)
        ct1[0:AOUT, :] = new1.astype(BF16).astype(F32) * (row_ok * mask1)
        of_global1(t).wait_send()
        of_global2(t).wait_send()
        of_halo(t).wait_send()
        return carry

    lax.fori_loop(1, PHASES, iteration, 0)


def solution(mesh):
    ns, nn = mesh.shape["stripe"], mesh.shape["scan"]

    def per_device(dose, target, psf):
        vmem = pl.BlockSpec(memory_space=pltpu.VMEM)
        f = lambda *shape: pltpu.VMEM(shape, F32)
        h = lambda *shape: pltpu.VMEM(shape, BF16)
        return pl.pallas_call(
            lambda *refs: kernel(ns, nn, *refs),
            out_shape=(
                jax.ShapeDtypeStruct((TX, TY), F32),
                jax.ShapeDtypeStruct((TX, TY), F32),
            ),
            in_specs=[vmem] * 3,
            out_specs=(vmem, vmem),
            scratch_shapes=[
                f(PHASES, ns, 8, 128), f(PHASES, nn, 8, 128), h(PHASES, HALO, 128),
                h(SIDE, 128), h(EDGE, 128),
                f(EROWS, 128), f(EROWS, 128), f(CROWS, 128), f(CROWS, 128),
                f(AOUT, 128), f(AOUT, 128),
                h(8, 2048, 256), h(4, 2048, 256), h(144, 3200),
                f(64, 128), f(64, 128), f(64, 128), f(128, 128),
                h(AIN, 2048), h(BIN, 2048),
                f(TX, 128), f(TX, 128), f(40, 128), f(16, 128),
                f(128, 128), f(nn * 8, 512), f(416, 128), f(416, 128), f(TX, 128),
                pltpu.SemaphoreType.DMA((3,)), pltpu.SemaphoreType.DMA((PHASES, 3)),
            ],
            compiler_params=pltpu.CompilerParams(
                collective_id=0, has_side_effects=True, vmem_limit_bytes=60 << 20
            ),
            name="dose",
        )(dose, target, psf)

    return jax.shard_map(
        per_device, mesh=mesh,
        in_specs=(P("stripe", "scan"), P("stripe", "scan"), P()),
        out_specs=(P("stripe", "scan"), P("stripe", "scan")),
        check_vma=False,
    )
```

profile of v0, /device:TPU:1, one launch (start us, length us, event | category | flops | bytes accessed | tf_op | source)
XLA Modules:
  0.0 82.7 jit_solution(1167555194000126641)
XLA Ops:
  0.6 79.8 %dose.1 = (f32[200,100]{1,0:T(8,128)}, f32[200,100]{1,0:T(8,128)}) custom-call(bf16[200,100]{1,0:T(8,128)(2,1)} %refs_0_.1, s32[200,100]{1,0:T(8,128)} %refs_1_.1, bf16[61,61]{1,0:T(8,128)(2,1)} %refs_2_.1), custom_call_target="tpu_custom_call" | custom-call | tf_op jit(solution)/shard_map/dose/pallas_call | solution.py:407
  80.5 0.0 copy-start
  80.5 1.6 %copy.7 = f32[200,100]{1,0:T(8,128)} copy(f32[200,100]{1,0:T(8,128)} %get-tuple-element.4) | data formatting | bytes 160000
  82.1 0.0 copy-done
  82.1 0.6 copy.8
Async XLA Ops:
  80.5 1.6 %copy-start = (f32[200,100]{1,0:T(8,128)S(1)}, f32[200,100]{1,0:T(8,128)}, u32[]{:S(2)}) copy-start(f32[200,100]{1,0:T(8,128)} %get-tuple-element.5) | copy-start | bytes 240004
where the time goes:
time: 82.8 us; the launch traced here: 82.7 us
  Pallas kernels  79.8 us (96%)
  local copies, waits for them, and re-layouts  2.22 us (3%)
    pallas_call x1, Pallas kernels, per_device(): pl.pallas_call(lambda *refs: kernel(ns, nn, *refs), out_shape=(jax.ShapeD...  79.8 us
    unnamed x4, local copies, waits for them, and re-layouts  2.22 us

commit v1 on v0

v1 whole, which is shorter than its diff:
```python
import math

import jax
import jax.numpy as jnp
from jax import lax
from jax.experimental import pallas as pl
from jax.experimental.pallas import tpu as pltpu
from jax.sharding import PartitionSpec as P

TX, TY = 200, 100
TAPS = 61
COARSE = 25
SIGMA = 40
ITERS = 4
RIM = 30
BACK = 0.6
GAIN = 3.0
LEVEL = 1.5
STEP = 0.5
CROW, CCOL = TX // COARSE, TY // COARSE
ADJ_SCALE = BACK / (COARSE * COARSE)

MESH = pl.DeviceIdType.MESH
F32, BF16 = jnp.float32, jnp.bfloat16
HI = lax.Precision.HIGHEST

EROWS = 336
CROWS = 272
AOUT = 264
AIN = 320
BIN = 256
PHASES = ITERS + 1
SIDE = 208
EDGE = 64
HALO = 2 * SIDE + 6 * EDGE


def iota(shape, dim):
    return lax.broadcasted_iota(jnp.int32, shape, dim)


def dot(a, b, precision=None):
    return jnp.dot(a, b, precision=precision, preferred_element_type=F32)


def dot_nt(a, b, precision=None):
    return lax.dot_general(
        a, b, (((1,), (1,)), ((), ())), precision=precision, preferred_element_type=F32
    )


def gauss(dist):
    d = dist.astype(F32)
    return jnp.exp(-d * d / (2.0 * SIGMA * SIGMA)) / (math.sqrt(2.0 * math.pi) * SIGMA)


def cell_of(col):
    out = jnp.full(col.shape, -3, jnp.int32)
    for k in range(-2, 7):
        out = out + jnp.where(col >= COARSE * k, 1, 0)
    return out


def kernel(
    ns, nn, dose_ref, target_ref, psf_ref, resist_ref, updated_ref,
    g1, g2, halo, tile, bottom, et0, et1, ct0, ct1, at0, at1, wa, wf, vv,
    ps, rf, ra, fr, xa, xb, err, own, zs, sc, mw, cu, ub0, ub1, bk, bl,
    send_sem, recv_sem,
):
    s = lax.axis_index("stripe")
    n = lax.axis_index("scan")
    ncx, ncy = ns * CROW, nn * CCOL
    up, down = lax.rem(s + ns - 1, ns), lax.rem(s + 1, ns)
    left, right = lax.rem(n + nn - 1, nn), lax.rem(n + 1, nn)

    far = lambda count: sorted(range(1, count), key=lambda k: -min(k, count - k))
    barrier = pltpu.get_barrier_semaphore()

    def hello(a, b):
        pl.semaphore_signal(barrier, inc=1, device_id=(a, b), device_id_type=MESH)

    for a in (up, down):
        for b in (left, right):
            hello(a, b)
    for k in far(nn):
        hello(s, lax.rem(n + k, nn))
    for k in far(ns):
        hello(lax.rem(s + k, ns), n)

    lane = iota((1, 128), 1)

    def field_out(value):
        tile[0:TX, :] = value.astype(BF16)
        bottom[...] = value[TX - EDGE:, :].astype(BF16)

    def col_sum(ref):
        total = ref[pl.ds(0, CROW, stride=COARSE), :]
        for u in range(1, COARSE):
            total = total + ref[pl.ds(u, CROW, stride=COARSE), :]
        return total

    pick_row = iota((8, 128), 0)
    pick_cell = cell_of(iota((8, 128), 1))
    pick_in = iota((8, 128), 1) < TY
    pick_sum = jnp.where((pick_cell == pick_row) & pick_in, 1.0, 0.0)
    pick_dose = jnp.where((pick_cell == pick_row - 2) & pick_in, 1.0, 0.0)
    zs[...] = jnp.zeros_like(zs)
    sc[...] = jnp.zeros_like(sc)

    def sums_out(err_cols):
        sc[0:8, 0:8] = dot_nt(pick_sum, err_cols, HI)
        return pltpu.roll(jnp.where(lane < CROW, sc[0:8, :], 0.0), s * CROW, 1)

    def cells_out(cur_cols, spread):
        sc[8:16, 0:8] = dot_nt(pick_dose, cur_cols, HI)
        cells = pltpu.roll(jnp.where(lane < CROW, sc[8:16, :], 0.0), 64 + s * CROW, 1)
        cells = cells * (1.0 / (COARSE * COARSE))
        if spread is not None:
            zs[:, 0:8] = spread
            part = jnp.zeros((8, 128), F32)
            for d in range(5):
                part = part + pltpu.roll(zs[8 * d:8 * d + 8, :], 62 + d + s * CROW, 1)
            cells = cells - (STEP / (COARSE * COARSE)) * part
        return jnp.where(lane < 64, 0.0, cells)

    def start_stage1(which, t, value):
        g1[which, t, s] = value
        for k in far(ns):
            pltpu.make_async_remote_copy(
                g1.at[which, t, s], g1.at[which, t, s], send_sem.at[which], recv_sem.at[t, which],
                device_id=(lax.rem(s + k, ns), n), device_id_type=MESH,
            ).start()

    def start_stage2(which, t, value):
        g2[which, t, n] = value
        for k in far(nn):
            pltpu.make_async_remote_copy(
                g2.at[which, t, n], g2.at[which, t, n], send_sem.at[2 + which], recv_sem.at[t, 2 + which],
                device_id=(s, lax.rem(n + k, nn)), device_id_type=MESH,
            ).start()

    def start_halo(t):
        def go(src, first, rows, a, b):
            pltpu.make_async_remote_copy(
                src, halo.at[t, pl.ds(first, rows)], send_sem.at[4], recv_sem.at[t, 4],
                device_id=(a, b), device_id_type=MESH,
            ).start()

        top = tile.at[pl.ds(0, EDGE)]
        first = 2 * SIDE
        go(bottom, first + 2 * EDGE, EDGE, down, right)
        go(bottom, first + 3 * EDGE, EDGE, down, left)
        go(top, first + 4 * EDGE, EDGE, up, right)
        go(top, first + 5 * EDGE, EDGE, up, left)
        go(bottom, first, EDGE, down, n)
        go(top, first + EDGE, EDGE, up, n)
        go(tile, 0, SIDE, s, right)
        go(tile, SIDE, SIDE, s, left)

    def all_of(ref, sem_send, sem_recv):
        return pltpu.make_async_remote_copy(
            ref, ref, sem_send, sem_recv, device_id=(s, right), device_id_type=MESH
        )

    def of_stage1(which, t):
        return all_of(g1.at[which, t, pl.ds(0, ns - 1)], send_sem.at[which], recv_sem.at[t, which])

    def of_stage2(which, t):
        return all_of(g2.at[which, t, pl.ds(0, nn - 1)], send_sem.at[2 + which], recv_sem.at[t, 2 + which])

    def of_halo(t):
        return all_of(halo.at[t], send_sem.at[4], recv_sem.at[t, 4])

    def assemble(t, centre):
        yes = lambda c: jnp.where(c, 1.0, 0.0).astype(F32)
        has_up, has_down = yes(s > 0), yes(s < ns - 1)
        has_left, has_right = yes(n > 0), yes(n < nn - 1)
        first = 2 * SIDE

        def band(row, rows, mid, lhs, rhs, flag):
            lhs = pltpu.roll(lhs, 28, 1) * (has_left * flag)
            rhs = pltpu.roll(rhs, TY, 1) * (has_right * flag)
            et0[row:row + rows, :] = jnp.where(lane < TY, mid * flag, rhs)
            et1[row:row + rows, :] = jnp.where(lane < 32, rhs, jnp.where(lane >= 68, lhs, 0.0))

        def part(k, rows):
            return halo[t, pl.ds(k, rows), :].astype(F32)

        band(0, EDGE, part(first, EDGE), part(first + 2 * EDGE, EDGE), part(first + 3 * EDGE, EDGE), has_up)
        band(EDGE, TX, centre, part(0, TX), part(SIDE, TX), jnp.float32(1.0))
        band(EDGE + TX, EDGE, part(first + EDGE, EDGE), part(first + 4 * EDGE, EDGE), part(first + 5 * EDGE, EDGE), has_down)

    def rows_result(which, t):
        total = g1[which, t, 0]
        for k in range(1, ns):
            total = total + g1[which, t, k]
        parts = []
        for _ in range(3):
            parts.append(total.astype(BF16).astype(F32))
            total = total - parts[-1]
        parts.append(jnp.zeros_like(total))
        p = dot(jnp.concatenate(parts, axis=0).astype(BF16), mw[...])
        out = p[16:24, 0:128] + p[8:16, 128:256] + p[0:8, 256:384]
        out = out + p[8:16, 0:128] + p[0:8, 128:256]
        out = out + p[0:8, 0:128]
        row = iota((8, 128), 0)
        out = jnp.where(jnp.bitwise_and(row, 3) == iota((8, 128), 1) // 32, out, 0.0)
        return jnp.concatenate(
            [jnp.sum(out[0:4], axis=0, keepdims=True), jnp.sum(out[4:8], axis=0, keepdims=True)], axis=0)

    def turned_back(which, t):
        stack = jnp.concatenate([g2[which, t].reshape(nn * 2, 128), jnp.zeros((64, 128), F32)], axis=0)
        turned = jnp.transpose(stack)
        return jnp.concatenate(
            [turned[0:32] + pltpu.roll(turned[32:64], 64, 1), turned[64:96] + pltpu.roll(turned[96:128], 64, 1)],
            axis=1)

    def set_back(t, from_sums):
        value = dot(turned_back(1, t)[24:32], cu[:, 384:512], HI)
        value = BACK * (value if from_sums is None else value + from_sums)
        for u in range(COARSE):
            bk[pl.ds(u, CROW, stride=COARSE), :] = value

    def blur():
        for k in range(8):
            xb[:, 256 * k:256 * k + 128] = ct0[k + 2:k + 2 + BIN, :].astype(BF16)
            xb[:, 256 * k + 128:256 * k + 256] = ct1[k + 2:k + 2 + BIN, :].astype(BF16)
        blurred = None
        for pair in range(4):
            piece = dot(xb[...], wf[pair])
            lo = 16 * pair
            both = piece[lo:lo + TX, 0:128] + piece[lo + 8:lo + 8 + TX, 128:256]
            blurred = both if blurred is None else blurred + both
        bl[...] = blurred

    ps[...] = jnp.zeros_like(ps)
    ps[0:TAPS, 0:TAPS] = psf_ref[...].astype(F32)
    taps = ps[...]
    taps_h = taps.astype(BF16)
    b_at, l_at = iota((128, 128), 0), iota((128, 128), 1)
    perm_f = jnp.where((l_at == lax.rem(RIM - b_at + 256, 128)) & (b_at < TAPS), 1.0, 0.0).astype(BF16)
    perm_a = jnp.where((l_at == lax.rem(b_at - RIM + 256, 128)) & (b_at < TAPS), 1.0, 0.0).astype(BF16)
    flip = jnp.where(iota((64, 64), 1) == TAPS - 1 - iota((64, 64), 0), 1.0, 0.0).astype(BF16)
    rf[...] = dot(taps_h, perm_f)
    ra[...] = dot(dot(flip, taps_h).astype(BF16), perm_a)

    dose = jnp.zeros((TX, 128), F32)
    own[...] = dose
    own[:, 0:TY] = dose_ref[...].astype(F32)
    tile[...] = jnp.zeros_like(tile)
    field_out(own[...])
    first_payload = cells_out(col_sum(own), None)

    g_row = jnp.bitwise_and(b_at, 63)
    l32 = jnp.bitwise_and(l_at, 31)
    full_rows = gauss(iota((ncx, ncx), 0) - iota((ncx, ncx), 1))
    l64 = jnp.bitwise_and(iota((ncx, 128), 1), 31)
    twice = dot(full_rows, gauss(iota((ncx, 128), 0) - (s * CROW + l64 - 16)), HI)
    upper = jnp.concatenate([twice, jnp.zeros((128 - ncx, 128), F32)], axis=0)
    low = b_at < 64
    table = jnp.where(low & (l32 < 12), gauss(g_row - (s * CROW + l32 - 2)), 0.0)
    table = table + jnp.where(low & (l32 >= 16) & (l32 < 24), upper, 0.0)
    table = table + jnp.where((~low) & (l32 >= 24), gauss(g_row - (s * CROW + l32 - 24)), 0.0)
    table = jnp.where(g_row < ncx, table, 0.0)
    for k in range(3):
        rounded = table.astype(BF16)
        mw[:, 128 * k:128 * k + 128] = rounded
        table = table - rounded.astype(F32)
    mw[:, 384:512] = jnp.zeros((128, 128), BF16)

    k_at, a_at = iota((128, 64), 0), iota((128, 64), 1)
    u_at = k_at // 5
    low_a = COARSE * (k_at - 5 * u_at - 2) - u_at + RIM
    rows_w = jnp.where((a_at >= low_a) & (a_at < low_a + COARSE), 1.0, 0.0).astype(BF16)
    x_at = -2 * COARSE - jnp.where(l_at < 16, l_at, l_at - 128)
    cols_w = jnp.where((b_at >= x_at + RIM) & (b_at < x_at + RIM + COARSE), 1.0, 0.0)
    fr[...] = dot(dot(rows_w, taps_h), cols_w, HI)
    j8 = iota((8, 128), 0)
    c8 = iota((8, 128), 1)
    xx = COARSE * (j8 - 2) - c8
    inside = (xx >= RIM - 84) & (xx <= RIM) & (c8 < TY)
    for u in range(COARSE):
        pieces = []
        for d in range(5):
            row = jnp.broadcast_to(fr[5 * u + d:5 * u + d + 1, :], (8, 128))
            row = pltpu.roll(pltpu.roll(row, 0, 1, stride=12, stride_axis=0), 0, 1, stride=13, stride_axis=0)
            pieces.append(jnp.where(inside, row, 0.0))
        for d in range(5):
            top = pieces[d].astype(BF16).astype(F32)
            both = jnp.concatenate([top, pieces[d] - top], axis=0).astype(BF16)
            vv[16 * d:16 * d + 16, 128 * u:128 * u + 128] = both

    pl.semaphore_wait(barrier, ns - 1 + nn - 1 + 4)
    start_stage1(1, 0, first_payload)
    start_halo(0)

    near = jnp.abs(b_at - l_at) <= RIM

    def circulant(row):
        full = pltpu.roll(jnp.broadcast_to(row, (128, 128)), 0, 1, stride=1, stride_axis=0)
        return jnp.where(near, full, 0.0).astype(BF16), jnp.where(near, 0.0, full).astype(BF16)

    def one_pair(k, carry):
        pair, shift = k // 8, lax.rem(k, 8)
        at_row = pl.multiple_of(shift * 256, 256)
        for half in range(2):
            tap = pair * 16 + half * 8 + shift
            same, other = circulant(rf[pl.ds(tap, 1), :])
            wf[pair, pl.ds(at_row, 128), half * 128:half * 128 + 128] = same
            wf[pair, pl.ds(at_row + 128, 128), half * 128:half * 128 + 128] = other
            same, other = circulant(ra[pl.ds(tap, 1), :])
            group = pair * 2 + half
            wa[group, pl.ds(at_row, 128), 0:128] = same
            wa[group, pl.ds(at_row, 128), 128:256] = other
            wa[group, pl.ds(at_row + 128, 128), 0:128] = other
            wa[group, pl.ds(at_row + 128, 128), 128:256] = same
        return carry

    lax.fori_loop(0, 32, one_pair, 0)

    of_stage1(1, 0).wait_recv()
    start_stage2(1, 0, rows_result(1, 0))

    rows8 = nn * 8

    def q_dev(shape):
        at = iota(shape, 0)
        return 4 * jnp.bitwise_and(at, 1) + at // 64, jnp.bitwise_and(at, 63) // 2

    q, dev = q_dev((rows8, 256))
    pos = iota((rows8, 256), 1)
    col = jnp.where(pos < 160, pos, pos - 256)
    cu[:, 0:256] = jnp.where(q < CCOL, gauss(CCOL * dev + q - (CCOL * n + cell_of(col))), 0.0)
    q1, dev1 = q[:, 0:128], dev[:, 0:128]
    lane_cell = CCOL * n + cell_of(iota((rows8, 128), 1))
    mid_at = iota((ncy, 128), 0)
    mid = gauss(mid_at - (CCOL * n + cell_of(iota((ncy, 128), 1))))
    qf, devf = q_dev((rows8, ncy))
    outer = jnp.where(qf < CCOL, gauss(CCOL * (devf) + qf - iota((rows8, ncy), 1)), 0.0)
    cu[:, 256:384] = (-STEP * ADJ_SCALE) * dot(outer, mid, HI)
    at = CCOL * dev1 + q1 - 2
    cu[:, 384:512] = jnp.where((at >= 0) & (at < ncy), gauss(at - lane_cell), 0.0)


    et0[AIN + 8:, :] = jnp.zeros((EROWS - AIN - 8, 128), F32)
    et1[AIN + 8:, :] = jnp.zeros((EROWS - AIN - 8, 128), F32)
    ct0[AOUT:, :] = jnp.zeros((CROWS - AOUT, 128), F32)
    ct1[AOUT:, :] = jnp.zeros((CROWS - AOUT, 128), F32)

    of_halo(0).wait_recv()
    assemble(0, own[...])
    ct0[0:AOUT, :] = et0[32:32 + AOUT, :]
    ct1[0:AOUT, :] = et1[32:32 + AOUT, :]

    blur()
    of_stage2(1, 0).wait_recv()
    set_back(0, None)
    of_stage1(1, 0).wait_send()
    of_stage2(1, 0).wait_send()
    of_halo(0).wait_send()

    yes = lambda c: jnp.where(c, 1.0, 0.0).astype(F32)
    row_ok = jnp.ones((AOUT, 1), F32)
    r_at = iota((AOUT, 1), 0) - 32
    row_ok = jnp.where(r_at < 0, yes(s > 0), jnp.where(r_at >= TX, yes(s < ns - 1), 1.0))
    mask0 = jnp.where(lane < TY, 1.0, yes(n < nn - 1))
    mask1 = jnp.where(lane < 32, yes(n < nn - 1), yes(n > 0))

    def iteration(t, carry):
        exposure = bl[...] + bk[...]
        resist = jax.nn.sigmoid(GAIN * (exposure - LEVEL))
        own[:, 0:TY] = target_ref[...].astype(F32)
        error = (resist - own[...]) * GAIN * resist * (1.0 - resist)
        error = jnp.where(lane < TY, error, 0.0)
        err[...] = error
        half = error.astype(BF16).astype(F32)
        own[...] = half
        field_out(half)
        resist_ref[...] = resist[:, 0:TY]

        start_stage1(0, t, sums_out(col_sum(err)))
        start_halo(t)

        @pl.when(t < ITERS)
        def _():
            cells_in = jnp.concatenate(
                [own[pl.ds(u, CROW, stride=COARSE), :].astype(BF16) for u in range(COARSE)], axis=1)
            two = dot_nt(vv[...], cells_in)
            spread = jnp.concatenate([two[16 * d:16 * d + 8] + two[16 * d + 8:16 * d + 16] for d in range(5)], axis=0)
            cur_cols = jnp.where(lane < TY, col_sum(ct0.at[pl.ds(32, TX)]), 0.0)
            start_stage1(1, t, cells_out(cur_cols, spread))

        of_stage1(0, t).wait_recv()
        start_stage2(0, t, rows_result(0, t))

        @pl.when(t < ITERS)
        def _():
            of_stage1(1, t).wait_recv()
            start_stage2(1, t, rows_result(1, t))

        of_halo(t).wait_recv()
        assemble(t, own[...])
        for k in range(8):
            xa[:, 256 * k:256 * k + 128] = et0[k + 2:k + 2 + AIN, :].astype(BF16)
            xa[:, 256 * k + 128:256 * k + 256] = et1[k + 2:k + 2 + AIN, :].astype(BF16)
        for group in range(8):
            piece = dot(xa[...], wa[group])
            lo = 8 * group
            if group == 0:
                at0[...] = piece[lo:lo + AOUT, 0:128]
                at1[...] = piece[lo:lo + AOUT, 128:256]
            else:
                at0[...] += piece[lo:lo + AOUT, 0:128]
                at1[...] += piece[lo:lo + AOUT, 128:256]

        of_stage2(0, t).wait_recv()
        out = dot(turned_back(0, t), cu[:, 0:384], HI)
        for u in range(COARSE):
            for ref, first in ((ub0, 0), (ub1, 128)):
                ref[pl.ds(6 + u, 8, stride=COARSE), :] = out[0:8, first:first + 128]
                ref[pl.ds(206 + u, 8, stride=COARSE), :] = out[8:16, first:first + 128]
        new0 = ct0[0:AOUT, :] - STEP * (at0[...] + ADJ_SCALE * ub0[24:24 + AOUT, :])
        new1 = ct1[0:AOUT, :] - STEP * (at1[...] + ADJ_SCALE * ub1[24:24 + AOUT, :])
        updated_ref[...] = new0[32:32 + TX, 0:TY]
        ct0[0:AOUT, :] = new0.astype(BF16).astype(F32) * (row_ok * mask0)
        ct1[0:AOUT, :] = new1.astype(BF16).astype(F32) * (row_ok * mask1)

        @pl.when(t < ITERS)
        def _():
            blur()
            of_stage2(1, t).wait_recv()
            set_back(t, out[16:24, 256:384])
            of_stage1(1, t).wait_send()
            of_stage2(1, t).wait_send()

        of_stage1(0, t).wait_send()
        of_stage2(0, t).wait_send()
        of_halo(t).wait_send()
        return carry

    lax.fori_loop(1, PHASES, iteration, 0)


def solution(mesh):
    ns, nn = mesh.shape["stripe"], mesh.shape["scan"]

    def per_device(dose, target, psf):
        vmem = pl.BlockSpec(memory_space=pltpu.VMEM)
        f = lambda *shape: pltpu.VMEM(shape, F32)
        h = lambda *shape: pltpu.VMEM(shape, BF16)
        return pl.pallas_call(
            lambda *refs: kernel(ns, nn, *refs),
            out_shape=(
                jax.ShapeDtypeStruct((TX, TY), F32),
                jax.ShapeDtypeStruct((TX, TY), F32),
            ),
            in_specs=[vmem] * 3,
            out_specs=(vmem, vmem),
            scratch_shapes=[
                f(2, PHASES, ns, 8, 128), f(2, PHASES, nn, 2, 128), h(PHASES, HALO, 128),
                h(SIDE, 128), h(EDGE, 128),
                f(EROWS, 128), f(EROWS, 128), f(CROWS, 128), f(CROWS, 128),
                f(AOUT, 128), f(AOUT, 128),
                h(8, 2048, 256), h(4, 2048, 256), h(80, 3200),
                f(64, 128), f(64, 128), f(64, 128), f(128, 128),
                h(AIN, 2048), h(BIN, 2048),
                f(TX, 128), f(TX, 128), f(40, 128), f(16, 128),
                h(128, 512), f(nn * 8, 512), f(416, 128), f(416, 128), f(TX, 128), f(TX, 128),
                pltpu.SemaphoreType.DMA((5,)), pltpu.SemaphoreType.DMA((PHASES, 5)),
            ],
            compiler_params=pltpu.CompilerParams(
                collective_id=0, has_side_effects=True, vmem_limit_bytes=60 << 20
            ),
            name="dose",
        )(dose, target, psf)

    return jax.shard_map(
        per_device, mesh=mesh,
        in_specs=(P("stripe", "scan"), P("stripe", "scan"), P()),
        out_specs=(P("stripe", "scan"), P("stripe", "scan")),
        check_vma=False,
    )
```

time: 82.8 us -> 76.4 us (0.923)
  Pallas kernels: 79.8 us -> 73.4 us
    pallas_call x1, Pallas kernels: 79.8 us -> 73.4 us  [per_device(): pl.pallas_call(lambda *refs: kernel(ns, nn, *refs), out_shape=(jax.ShapeD...]
where the time goes in v1:
time: 76.4 us; the launch traced here: 76.3 us
  Pallas kernels  73.4 us (96%)
  local copies, waits for them, and re-layouts  2.22 us (3%)
    pallas_call x1, Pallas kernels, per_device(): pl.pallas_call(lambda *refs: kernel(ns, nn, *refs), out_shape=(jax.ShapeD...  73.4 us
    unnamed x4, local copies, waits for them, and re-layouts  2.22 us

profile of v1, /device:TPU:1, one launch (start us, length us, event | category | flops | bytes accessed | tf_op | source)
XLA Modules:
  0.0 76.3 jit_solution(4271607249515863082)
XLA Ops:
  0.6 73.4 %dose.1 = (f32[200,100]{1,0:T(8,128)}, f32[200,100]{1,0:T(8,128)}) custom-call(bf16[200,100]{1,0:T(8,128)(2,1)} %refs_0_.1, s32[200,100]{1,0:T(8,128)} %refs_1_.1, bf16[61,61]{1,0:T(8,128)(2,1)} %refs_2_.1), custom_call_target="tpu_custom_call" | custom-call | tf_op jit(solution)/shard_map/dose/pallas_call | solution.py:451
  74.0 0.0 copy-start
  74.1 1.6 %copy.7 = f32[200,100]{1,0:T(8,128)} copy(f32[200,100]{1,0:T(8,128)} %get-tuple-element.4) | data formatting | bytes 160000
  75.6 0.0 copy-done
  75.6 0.6 copy.8
Async XLA Ops:
  74.0 1.6 %copy-start = (f32[200,100]{1,0:T(8,128)S(1)}, f32[200,100]{1,0:T(8,128)}, u32[]{:S(2)}) copy-start(f32[200,100]{1,0:T(8,128)} %get-tuple-element.5) | copy-start | bytes 240004

commit v2 on v1

--- a/solution.py
+++ b/solution.py
@@ -30,9 +30,13 @@
 AIN = 320
 BIN = 256
 PHASES = ITERS + 1
-SIDE = 208
+SIDE = 112
+SIDE_ROWS = 104
+CORNER = 32
 EDGE = 64
-HALO = 2 * SIDE + 6 * EDGE
+AT = (0, SIDE, 2 * SIDE, 2 * SIDE + CORNER, 2 * SIDE + 2 * CORNER, 2 * SIDE + 3 * CORNER,
+      2 * SIDE + 4 * CORNER, 2 * SIDE + 4 * CORNER + EDGE)
+HALO = 2 * SIDE + 4 * CORNER + 2 * EDGE
 
 
 def iota(shape, dim):
@@ -63,8 +67,8 @@
 
 def kernel(
     ns, nn, dose_ref, target_ref, psf_ref, resist_ref, updated_ref,
-    g1, g2, halo, tile, bottom, et0, et1, ct0, ct1, at0, at1, wa, wf, vv,
-    ps, rf, ra, fr, xa, xb, err, own, zs, sc, mw, cu, ub0, ub1, bk, bl,
+    g1, g2, halo, tile, et0, et1, ct0, ct1, at0, at1, wa, wf, vv,
+    ps, rf, ra, fr, xa, xb, err, own, zs, sc, mw, cu, cb, ub0, ub1, bk, bl,
     send_sem, recv_sem,
 ):
     s = lax.axis_index("stripe")
@@ -73,7 +77,19 @@
     up, down = lax.rem(s + ns - 1, ns), lax.rem(s + 1, ns)
     left, right = lax.rem(n + nn - 1, nn), lax.rem(n + 1, nn)
 
-    far = lambda count: sorted(range(1, count), key=lambda k: -min(k, count - k))
+    x_lo = lax.rem(n // 2, 2)
+    core = lax.rem(n, 2)
+    far = lambda count: sorted(range(count), key=lambda k: -min(k, count - k))
+    plane, column = [], []
+    for k in far(ns):
+        for flip in (1, 0):
+            if k or flip:
+                plane.append((lax.rem(s + k, ns), n + 2 * flip * (1 - 2 * x_lo)))
+    for k in far(nn // 4):
+        for flip in (1, 0):
+            if k or flip:
+                column.append((s, lax.rem(n + 4 * k, nn) + flip * (1 - 2 * core)))
+    own1, own2 = x_lo * ns + s, (n // 4) * 2 + core
     barrier = pltpu.get_barrier_semaphore()
 
     def hello(a, b):
@@ -82,16 +98,28 @@
     for a in (up, down):
         for b in (left, right):
             hello(a, b)
-    for k in far(nn):
-        hello(s, lax.rem(n + k, nn))
-    for k in far(ns):
-        hello(lax.rem(s + k, ns), n)
+    for b in (left, right):
+        hello(s, b)
+    for a, b in plane + column:
+        hello(a, b)
 
     lane = iota((1, 128), 1)
 
+    def fold(value):
+        half = value.shape[0] // 2
+        return jnp.where(lane < 64, value[0:half], pltpu.roll(value[half:], 64, 1)).astype(BF16)
+
     def field_out(value):
-        tile[0:TX, :] = value.astype(BF16)
-        bottom[...] = value[TX - EDGE:, :].astype(BF16)
+        last = pltpu.roll(value, 92, 1)
+        more = jnp.zeros((2 * SIDE_ROWS - TX, 128), F32)
+        tile[AT[0]:AT[0] + SIDE_ROWS, :] = fold(jnp.concatenate([last, more], axis=0))
+        tile[AT[1]:AT[1] + SIDE_ROWS, :] = fold(jnp.concatenate([value, more], axis=0))
+        tile[AT[2]:AT[2] + CORNER, :] = fold(last[TX - EDGE:])
+        tile[AT[3]:AT[3] + CORNER, :] = fold(value[TX - EDGE:])
+        tile[AT[4]:AT[4] + CORNER, :] = fold(last[0:EDGE])
+        tile[AT[5]:AT[5] + CORNER, :] = fold(value[0:EDGE])
+        tile[AT[6]:AT[6] + EDGE, :] = value[TX - EDGE:].astype(BF16)
+        tile[AT[7]:AT[7] + EDGE, :] = value[0:EDGE].astype(BF16)
 
     def col_sum(ref):
         total = ref[pl.ds(0, CROW, stride=COARSE), :]
@@ -108,8 +136,16 @@
     sc[...] = jnp.zeros_like(sc)
 
     def sums_out(err_cols):
-        sc[0:8, 0:8] = dot_nt(pick_sum, err_cols, HI)
-        return pltpu.roll(jnp.where(lane < CROW, sc[0:8, :], 0.0), s * CROW, 1)
+        parts = []
+        for _ in range(3):
+            parts.append(err_cols.astype(BF16).astype(F32))
+            err_cols = err_cols - parts[-1]
+        parts.append(jnp.zeros_like(err_cols))
+        picks = jnp.concatenate([pick_sum, jnp.zeros_like(pick_sum)], axis=0).astype(BF16)
+        sc[:, 0:32] = dot_nt(picks, jnp.concatenate(parts, axis=0).astype(BF16))
+        got = sc[0:8, :]
+        got = got + (pltpu.roll(got, 128 - CROW, 1) + pltpu.roll(got, 128 - 2 * CROW, 1))
+        return pltpu.roll(jnp.where(lane < CROW, got, 0.0), s * CROW, 1)
 
     def cells_out(cur_cols, spread):
         sc[8:16, 0:8] = dot_nt(pick_dose, cur_cols, HI)
@@ -124,38 +160,30 @@
         return jnp.where(lane < 64, 0.0, cells)
 
     def start_stage1(which, t, value):
-        g1[which, t, s] = value
-        for k in far(ns):
+        g1[which, t, own1] = value
+        for a, b in plane:
             pltpu.make_async_remote_copy(
-                g1.at[which, t, s], g1.at[which, t, s], send_sem.at[which], recv_sem.at[t, which],
-                device_id=(lax.rem(s + k, ns), n), device_id_type=MESH,
-            ).start()
-
-    def start_stage2(which, t, value):
-        g2[which, t, n] = value
-        for k in far(nn):
-            pltpu.make_async_remote_copy(
-                g2.at[which, t, n], g2.at[which, t, n], send_sem.at[2 + which], recv_sem.at[t, 2 + which],
-                device_id=(s, lax.rem(n + k, nn)), device_id_type=MESH,
-            ).start()
-
-    def start_halo(t):
-        def go(src, first, rows, a, b):
-            pltpu.make_async_remote_copy(
-                src, halo.at[t, pl.ds(first, rows)], send_sem.at[4], recv_sem.at[t, 4],
+                g1.at[which, t, own1], g1.at[which, t, own1], send_sem.at[which], recv_sem.at[t, which],
                 device_id=(a, b), device_id_type=MESH,
             ).start()
 
-        top = tile.at[pl.ds(0, EDGE)]
-        first = 2 * SIDE
-        go(bottom, first + 2 * EDGE, EDGE, down, right)
-        go(bottom, first + 3 * EDGE, EDGE, down, left)
-        go(top, first + 4 * EDGE, EDGE, up, right)
-        go(top, first + 5 * EDGE, EDGE, up, left)
-        go(bottom, first, EDGE, down, n)
-        go(top, first + EDGE, EDGE, up, n)
-        go(tile, 0, SIDE, s, right)
-        go(tile, SIDE, SIDE, s, left)
+    def start_stage2(which, t, value):
+        g2[which, t, own2] = value
+        for a, b in column:
+            pltpu.make_async_remote_copy(
+                g2.at[which, t, own2], g2.at[which, t, own2], send_sem.at[2 + which], recv_sem.at[t, 2 + which],
+                device_id=(a, b), device_id_type=MESH,
+            ).start()
+
+    def start_halo(t):
+        sizes = (SIDE, SIDE, CORNER, CORNER, CORNER, CORNER, EDGE, EDGE)
+        to = ((s, right), (s, left), (down, right), (down, left), (up, right), (up, left), (down, n), (up, n))
+        for k in (2, 3, 4, 5, 6, 7, 0, 1):
+            part = pl.ds(AT[k], sizes[k])
+            pltpu.make_async_remote_copy(
+                tile.at[part], halo.at[t, part], send_sem.at[4], recv_sem.at[t, 4],
+                device_id=to[k], device_id_type=MESH,
+            ).start()
 
     def all_of(ref, sem_send, sem_recv):
         return pltpu.make_async_remote_copy(
@@ -163,10 +191,10 @@
         )
 
     def of_stage1(which, t):
-        return all_of(g1.at[which, t, pl.ds(0, ns - 1)], send_sem.at[which], recv_sem.at[t, which])
+        return all_of(g1.at[which, t, pl.ds(0, 2 * ns - 1)], send_sem.at[which], recv_sem.at[t, which])
 
     def of_stage2(which, t):
-        return all_of(g2.at[which, t, pl.ds(0, nn - 1)], send_sem.at[2 + which], recv_sem.at[t, 2 + which])
+        return all_of(g2.at[which, t, pl.ds(0, nn // 2 - 1)], send_sem.at[2 + which], recv_sem.at[t, 2 + which])
 
     def of_halo(t):
         return all_of(halo.at[t], send_sem.at[4], recv_sem.at[t, 4])
@@ -175,38 +203,39 @@
         yes = lambda c: jnp.where(c, 1.0, 0.0).astype(F32)
         has_up, has_down = yes(s > 0), yes(s < ns - 1)
         has_left, has_right = yes(n > 0), yes(n < nn - 1)
-        first = 2 * SIDE
 
         def band(row, rows, mid, lhs, rhs, flag):
-            lhs = pltpu.roll(lhs, 28, 1) * (has_left * flag)
-            rhs = pltpu.roll(rhs, TY, 1) * (has_right * flag)
+            lhs = jnp.concatenate([pltpu.roll(lhs, 64, 1), lhs], axis=0)[0:rows] * (has_left * flag)
+            rhs = jnp.concatenate([pltpu.roll(rhs, TY, 1), pltpu.roll(rhs, 36, 1)], axis=0)[0:rows] * (has_right * flag)
             et0[row:row + rows, :] = jnp.where(lane < TY, mid * flag, rhs)
             et1[row:row + rows, :] = jnp.where(lane < 32, rhs, jnp.where(lane >= 68, lhs, 0.0))
 
         def part(k, rows):
-            return halo[t, pl.ds(k, rows), :].astype(F32)
-
-        band(0, EDGE, part(first, EDGE), part(first + 2 * EDGE, EDGE), part(first + 3 * EDGE, EDGE), has_up)
-        band(EDGE, TX, centre, part(0, TX), part(SIDE, TX), jnp.float32(1.0))
-        band(EDGE + TX, EDGE, part(first + EDGE, EDGE), part(first + 4 * EDGE, EDGE), part(first + 5 * EDGE, EDGE), has_down)
+            return halo[t, pl.ds(AT[k], rows), :].astype(F32)
+
+        band(0, EDGE, part(6, EDGE), part(2, CORNER), part(3, CORNER), has_up)
+        band(EDGE, TX, centre, part(0, SIDE_ROWS), part(1, SIDE_ROWS), jnp.float32(1.0))
+        band(EDGE + TX, EDGE, part(7, EDGE), part(4, CORNER), part(5, CORNER), has_down)
 
     def rows_result(which, t):
-        total = g1[which, t, 0]
-        for k in range(1, ns):
-            total = total + g1[which, t, k]
+        totals = []
+        for x in range(2):
+            total = g1[which, t, x * ns]
+            for k in range(1, ns):
+                total = total + g1[which, t, x * ns + k]
+            totals.append(total)
+        total = jnp.concatenate(totals, axis=0)
         parts = []
         for _ in range(3):
             parts.append(total.astype(BF16).astype(F32))
             total = total - parts[-1]
-        parts.append(jnp.zeros_like(total))
         p = dot(jnp.concatenate(parts, axis=0).astype(BF16), mw[...])
-        out = p[16:24, 0:128] + p[8:16, 128:256] + p[0:8, 256:384]
-        out = out + p[8:16, 0:128] + p[0:8, 128:256]
-        out = out + p[0:8, 0:128]
-        row = iota((8, 128), 0)
-        out = jnp.where(jnp.bitwise_and(row, 3) == iota((8, 128), 1) // 32, out, 0.0)
-        return jnp.concatenate(
-            [jnp.sum(out[0:4], axis=0, keepdims=True), jnp.sum(out[4:8], axis=0, keepdims=True)], axis=0)
+        out = p[32:48, 0:128] + p[16:32, 128:256] + p[0:16, 256:384]
+        out = out + p[16:32, 0:128] + p[0:16, 128:256]
+        out = out + p[0:16, 0:128]
+        row = iota((16, 128), 0)
+        out = jnp.where(jnp.bitwise_and(row, 3) == iota((16, 128), 1) // 32, out, 0.0)
+        return jnp.concatenate([jnp.sum(out[4 * k:4 * k + 4], axis=0, keepdims=True) for k in range(4)], axis=0)
 
     def turned_back(which, t):
         stack = jnp.concatenate([g2[which, t].reshape(nn * 2, 128), jnp.zeros((64, 128), F32)], axis=0)
@@ -215,8 +244,21 @@
             [turned[0:32] + pltpu.roll(turned[32:64], 64, 1), turned[64:96] + pltpu.roll(turned[96:128], 64, 1)],
             axis=1)
 
+    def dot_cols(lhs, first, last):
+        rows = lhs.shape[0]
+        parts = []
+        for _ in range(3):
+            parts.append(lhs.astype(BF16).astype(F32))
+            lhs = lhs - parts[-1]
+        p = dot(jnp.concatenate(parts, axis=0).astype(BF16), cb[0, :, first:last])
+        q2 = dot(jnp.concatenate(parts[0:2], axis=0).astype(BF16), cb[1, :, first:last])
+        q3 = dot(parts[0].astype(BF16), cb[2, :, first:last])
+        out = p[2 * rows:] + q2[rows:] + q3
+        out = out + p[rows:2 * rows] + q2[0:rows]
+        return out + p[0:rows]
+
     def set_back(t, from_sums):
-        value = dot(turned_back(1, t)[24:32], cu[:, 384:512], HI)
+        value = dot_cols(turned_back(1, t)[24:32], 384, 512)
         value = BACK * (value if from_sums is None else value + from_sums)
         for u in range(COARSE):
             bk[pl.ds(u, CROW, stride=COARSE), :] = value
@@ -290,7 +332,7 @@
             both = jnp.concatenate([top, pieces[d] - top], axis=0).astype(BF16)
             vv[16 * d:16 * d + 16, 128 * u:128 * u + 128] = both
 
-    pl.semaphore_wait(barrier, ns - 1 + nn - 1 + 4)
+    pl.semaphore_wait(barrier, len(plane) + len(column) + 6)
     start_stage1(1, 0, first_payload)
     start_halo(0)
 
@@ -325,7 +367,9 @@
 
     def q_dev(shape):
         at = iota(shape, 0)
-        return 4 * jnp.bitwise_and(at, 1) + at // 64, jnp.bitwise_and(at, 63) // 2
+        pos = jnp.bitwise_and(at, 63)
+        z, c, x = pos // 8, jnp.bitwise_and(pos // 4, 1), jnp.bitwise_and(pos // 2, 1)
+        return 4 * jnp.bitwise_and(at, 1) + at // 64, 4 * z + 2 * x + c
 
     q, dev = q_dev((rows8, 256))
     pos = iota((rows8, 256), 1)
@@ -340,6 +384,10 @@
     cu[:, 256:384] = (-STEP * ADJ_SCALE) * dot(outer, mid, HI)
     at = CCOL * dev1 + q1 - 2
     cu[:, 384:512] = jnp.where((at >= 0) & (at < ncy), gauss(at - lane_cell), 0.0)
+    rest = cu[...]
+    for k in range(3):
+        cb[k] = rest.astype(BF16)
+        rest = rest - cb[k].astype(F32)
 
 
     et0[AIN + 8:, :] = jnp.zeros((EROWS - AIN - 8, 128), F32)
@@ -379,8 +427,6 @@
         resist_ref[...] = resist[:, 0:TY]
 
         start_stage1(0, t, sums_out(col_sum(err)))
-        start_halo(t)
-
         @pl.when(t < ITERS)
         def _():
             cells_in = jnp.concatenate(
@@ -389,6 +435,8 @@
             spread = jnp.concatenate([two[16 * d:16 * d + 8] + two[16 * d + 8:16 * d + 16] for d in range(5)], axis=0)
             cur_cols = jnp.where(lane < TY, col_sum(ct0.at[pl.ds(32, TX)]), 0.0)
             start_stage1(1, t, cells_out(cur_cols, spread))
+
+        start_halo(t)
 
         of_stage1(0, t).wait_recv()
         start_stage2(0, t, rows_result(0, t))
@@ -414,7 +462,8 @@
                 at1[...] += piece[lo:lo + AOUT, 128:256]
 
         of_stage2(0, t).wait_recv()
-        out = dot(turned_back(0, t), cu[:, 0:384], HI)
+        turned = turned_back(0, t)
+        out = dot_cols(turned[0:16], 0, 256)
         for u in range(COARSE):
             for ref, first in ((ub0, 0), (ub1, 128)):
                 ref[pl.ds(6 + u, 8, stride=COARSE), :] = out[0:8, first:first + 128]
@@ -428,8 +477,9 @@
         @pl.when(t < ITERS)
         def _():
             blur()
+            from_sums = dot_cols(turned[16:24], 256, 384)
             of_stage2(1, t).wait_recv()
-            set_back(t, out[16:24, 256:384])
+            set_back(t, from_sums)
             of_stage1(1, t).wait_send()
             of_stage2(1, t).wait_send()
 
@@ -457,15 +507,15 @@
             in_specs=[vmem] * 3,
             out_specs=(vmem, vmem),
             scratch_shapes=[
-                f(2, PHASES, ns, 8, 128), f(2, PHASES, nn, 2, 128), h(PHASES, HALO, 128),
-                h(SIDE, 128), h(EDGE, 128),
+                f(2, PHASES, 2 * ns, 8, 128), f(2, PHASES, nn // 2, 4, 128), h(PHASES, HALO, 128),
+                h(HALO, 128),
                 f(EROWS, 128), f(EROWS, 128), f(CROWS, 128), f(CROWS, 128),
                 f(AOUT, 128), f(AOUT, 128),
                 h(8, 2048, 256), h(4, 2048, 256), h(80, 3200),
                 f(64, 128), f(64, 128), f(64, 128), f(128, 128),
                 h(AIN, 2048), h(BIN, 2048),
                 f(TX, 128), f(TX, 128), f(40, 128), f(16, 128),
-                h(128, 512), f(nn * 8, 512), f(416, 128), f(416, 128), f(TX, 128), f(TX, 128),
+                h(128, 512), f(nn * 8, 512), h(3, nn * 8, 512), f(416, 128), f(416, 128), f(TX, 128), f(TX, 128),
                 pltpu.SemaphoreType.DMA((5,)), pltpu.SemaphoreType.DMA((PHASES, 5)),
             ],
             compiler_params=pltpu.CompilerParams(

time: 76.4 us -> 73.1 us (0.957)
  Pallas kernels: 73.4 us -> 70.1 us
    pallas_call x1, Pallas kernels: 73.4 us -> 70.1 us  [per_device(): pl.pallas_call(lambda *refs: kernel(ns, nn, *refs), out_shape=(jax.ShapeD...]
where the time goes in v2:
time: 73.1 us; the launch traced here: 73 us
  Pallas kernels  70.1 us (96%)
  local copies, waits for them, and re-layouts  2.22 us (3%)
    pallas_call x1, Pallas kernels, per_device(): pl.pallas_call(lambda *refs: kernel(ns, nn, *refs), out_shape=(jax.ShapeD...  70.1 us
    unnamed x4, local copies, waits for them, and re-layouts  2.22 us

profile of v2, /device:TPU:1, one launch (start us, length us, event | category | flops | bytes accessed | tf_op | source)
XLA Modules:
  0.0 73.0 jit_solution(3745420552303544876)
XLA Ops:
  0.6 70.1 %dose.1 = (f32[200,100]{1,0:T(8,128)}, f32[200,100]{1,0:T(8,128)}) custom-call(bf16[200,100]{1,0:T(8,128)(2,1)} %refs_0_.1, s32[200,100]{1,0:T(8,128)} %refs_1_.1, bf16[61,61]{1,0:T(8,128)(2,1)} %refs_2_.1), custom_call_target="tpu_custom_call" | custom-call | tf_op jit(solution)/shard_map/dose/pallas_call | solution.py:501
  70.8 0.0 copy-start
  70.8 1.6 %copy.7 = f32[200,100]{1,0:T(8,128)} copy(f32[200,100]{1,0:T(8,128)} %get-tuple-element.4) | data formatting | bytes 160000
  72.3 0.0 copy-done
  72.3 0.6 copy.8
Async XLA Ops:
  70.8 1.6 %copy-start = (f32[200,100]{1,0:T(8,128)S(1)}, f32[200,100]{1,0:T(8,128)}, u32[]{:S(2)}) copy-start(f32[200,100]{1,0:T(8,128)} %get-tuple-element.5) | copy-start | bytes 240004

commit v3 on v2

--- a/solution.py
+++ b/solution.py
@@ -66,9 +66,9 @@
 
 
 def kernel(
-    ns, nn, dose_ref, target_ref, psf_ref, resist_ref, updated_ref,
-    g1, g2, halo, tile, et0, et1, ct0, ct1, at0, at1, wa, wf, vv,
-    ps, rf, ra, fr, xa, xb, err, own, zs, sc, mw, cu, cb, ub0, ub1, bk, bl,
+    ns, nn, dose_ref, target_ref, psf_ref, both_ref,
+    gs1, gd1, gs2, gd2, halo, tile, et0, et1, ct0, ct1, at0, at1, wa, wf, vv,
+    ps, rf, ra, fr, xa, xb, err, own, zs, sc, mw, ts, td, ub0, ub1, bk, bl,
     send_sem, recv_sem,
 ):
     s = lax.axis_index("stripe")
@@ -145,7 +145,7 @@
         sc[:, 0:32] = dot_nt(picks, jnp.concatenate(parts, axis=0).astype(BF16))
         got = sc[0:8, :]
         got = got + (pltpu.roll(got, 128 - CROW, 1) + pltpu.roll(got, 128 - 2 * CROW, 1))
-        return pltpu.roll(jnp.where(lane < CROW, got, 0.0), s * CROW, 1)
+        return pltpu.roll(jnp.where(lane < CROW, got, 0.0), s * CROW, 1)[0:4]
 
     def cells_out(cur_cols, spread):
         sc[8:16, 0:8] = dot_nt(pick_dose, cur_cols, HI)
@@ -159,19 +159,23 @@
             cells = cells - (STEP / (COARSE * COARSE)) * part
         return jnp.where(lane < 64, 0.0, cells)
 
+    stage1, stage2 = (gs1, gd1), (gs2, gd2)
+
     def start_stage1(which, t, value):
-        g1[which, t, own1] = value
+        ref = stage1[which].at[t, own1]
+        ref[...] = value
         for a, b in plane:
             pltpu.make_async_remote_copy(
-                g1.at[which, t, own1], g1.at[which, t, own1], send_sem.at[which], recv_sem.at[t, which],
+                ref, ref, send_sem.at[which], recv_sem.at[t, which],
                 device_id=(a, b), device_id_type=MESH,
             ).start()
 
     def start_stage2(which, t, value):
-        g2[which, t, own2] = value
+        ref = stage2[which].at[t, own2]
+        ref[...] = value
         for a, b in column:
             pltpu.make_async_remote_copy(
-                g2.at[which, t, own2], g2.at[which, t, own2], send_sem.at[2 + which], recv_sem.at[t, 2 + which],
+                ref, ref, send_sem.at[2 + which], recv_sem.at[t, 2 + which],
                 device_id=(a, b), device_id_type=MESH,
             ).start()
 
@@ -191,10 +195,10 @@
         )
 
     def of_stage1(which, t):
-        return all_of(g1.at[which, t, pl.ds(0, 2 * ns - 1)], send_sem.at[which], recv_sem.at[t, which])
+        return all_of(stage1[which].at[t, pl.ds(0, 2 * ns - 1)], send_sem.at[which], recv_sem.at[t, which])
 
     def of_stage2(which, t):
-        return all_of(g2.at[which, t, pl.ds(0, nn // 2 - 1)], send_sem.at[2 + which], recv_sem.at[t, 2 + which])
+        return all_of(stage2[which].at[t, pl.ds(0, nn // 2 - 1)], send_sem.at[2 + which], recv_sem.at[t, 2 + which])
 
     def of_halo(t):
         return all_of(halo.at[t], send_sem.at[4], recv_sem.at[t, 4])
@@ -220,45 +224,55 @@
     def rows_result(which, t):
         totals = []
         for x in range(2):
-            total = g1[which, t, x * ns]
+            total = stage1[which][t, x * ns]
             for k in range(1, ns):
-                total = total + g1[which, t, x * ns + k]
+                total = total + stage1[which][t, x * ns + k]
             totals.append(total)
         total = jnp.concatenate(totals, axis=0)
+        rows = total.shape[0]
         parts = []
         for _ in range(3):
             parts.append(total.astype(BF16).astype(F32))
             total = total - parts[-1]
         p = dot(jnp.concatenate(parts, axis=0).astype(BF16), mw[...])
-        out = p[32:48, 0:128] + p[16:32, 128:256] + p[0:16, 256:384]
-        out = out + p[16:32, 0:128] + p[0:16, 128:256]
-        out = out + p[0:16, 0:128]
-        row = iota((16, 128), 0)
-        out = jnp.where(jnp.bitwise_and(row, 3) == iota((16, 128), 1) // 32, out, 0.0)
-        return jnp.concatenate([jnp.sum(out[4 * k:4 * k + 4], axis=0, keepdims=True) for k in range(4)], axis=0)
-
-    def turned_back(which, t):
-        stack = jnp.concatenate([g2[which, t].reshape(nn * 2, 128), jnp.zeros((64, 128), F32)], axis=0)
+        out = p[2 * rows:3 * rows, 0:128] + p[rows:2 * rows, 128:256] + p[0:rows, 256:384]
+        out = out + p[rows:2 * rows, 0:128] + p[0:rows, 128:256]
+        out = out + p[0:rows, 0:128]
+        row = iota((rows, 128), 0)
+        out = jnp.where(jnp.bitwise_and(row, 3) == iota((rows, 128), 1) // 32, out, 0.0)
+        return jnp.concatenate(
+            [jnp.sum(out[4 * k:4 * k + 4], axis=0, keepdims=True) for k in range(rows // 4)], axis=0)
+
+    def turned_sums(t):
+        stack = jnp.concatenate([gs2[t].reshape(nn, 128), jnp.zeros((128 - nn, 128), F32)], axis=0)
+        turned = jnp.transpose(stack)
+        out = turned[0:32]
+        for k in range(1, 4):
+            out = out + pltpu.roll(turned[32 * k:32 * k + 32], 32 * k, 1)
+        return out
+
+    def turned_cells(t):
+        stack = jnp.concatenate([gd2[t].reshape(nn * 2, 128), jnp.zeros((64, 128), F32)], axis=0)
         turned = jnp.transpose(stack)
         return jnp.concatenate(
             [turned[0:32] + pltpu.roll(turned[32:64], 64, 1), turned[64:96] + pltpu.roll(turned[96:128], 64, 1)],
             axis=1)
 
-    def dot_cols(lhs, first, last):
+    def dot_cols(lhs, table, first, last):
         rows = lhs.shape[0]
         parts = []
         for _ in range(3):
             parts.append(lhs.astype(BF16).astype(F32))
             lhs = lhs - parts[-1]
-        p = dot(jnp.concatenate(parts, axis=0).astype(BF16), cb[0, :, first:last])
-        q2 = dot(jnp.concatenate(parts[0:2], axis=0).astype(BF16), cb[1, :, first:last])
-        q3 = dot(parts[0].astype(BF16), cb[2, :, first:last])
+        p = dot(jnp.concatenate(parts, axis=0).astype(BF16), table[0, :, first:last])
+        q2 = dot(jnp.concatenate(parts[0:2], axis=0).astype(BF16), table[1, :, first:last])
+        q3 = dot(parts[0].astype(BF16), table[2, :, first:last])
         out = p[2 * rows:] + q2[rows:] + q3
         out = out + p[rows:2 * rows] + q2[0:rows]
         return out + p[0:rows]
 
     def set_back(t, from_sums):
-        value = dot_cols(turned_back(1, t)[24:32], 384, 512)
+        value = dot_cols(turned_cells(t)[24:32], td, 0, 128)
         value = BACK * (value if from_sums is None else value + from_sums)
         for u in range(COARSE):
             bk[pl.ds(u, CROW, stride=COARSE), :] = value
@@ -287,10 +301,10 @@
     ra[...] = dot(dot(flip, taps_h).astype(BF16), perm_a)
 
     dose = jnp.zeros((TX, 128), F32)
-    own[...] = dose
-    own[:, 0:TY] = dose_ref[...].astype(F32)
+    own[0:TX, :] = dose
+    own[0:TX, 0:TY] = dose_ref[...].astype(F32)
     tile[...] = jnp.zeros_like(tile)
-    field_out(own[...])
+    field_out(own[0:TX, :])
     first_payload = cells_out(col_sum(own), None)
 
     g_row = jnp.bitwise_and(b_at, 63)
@@ -363,31 +377,29 @@
     of_stage1(1, 0).wait_recv()
     start_stage2(1, 0, rows_result(1, 0))
 
-    rows8 = nn * 8
-
-    def q_dev(shape):
-        at = iota(shape, 0)
-        pos = jnp.bitwise_and(at, 63)
-        z, c, x = pos // 8, jnp.bitwise_and(pos // 4, 1), jnp.bitwise_and(pos // 2, 1)
-        return 4 * jnp.bitwise_and(at, 1) + at // 64, 4 * z + 2 * x + c
-
-    q, dev = q_dev((rows8, 256))
-    pos = iota((rows8, 256), 1)
+    def split(table, first, value):
+        for k in range(3):
+            rounded = value.astype(BF16)
+            table[k, :, first:first + value.shape[1]] = rounded
+            value = value - rounded.astype(F32)
+
+    def sum_col(width):
+        at = iota((nn * 4, width), 0)
+        z, c, x = jnp.bitwise_and(at, 31) // 4, jnp.bitwise_and(at // 2, 1), jnp.bitwise_and(at, 1)
+        return CCOL * (4 * z + 2 * x + c) + at // 32
+
+    pos = iota((nn * 4, 256), 1)
     col = jnp.where(pos < 160, pos, pos - 256)
-    cu[:, 0:256] = jnp.where(q < CCOL, gauss(CCOL * dev + q - (CCOL * n + cell_of(col))), 0.0)
-    q1, dev1 = q[:, 0:128], dev[:, 0:128]
-    lane_cell = CCOL * n + cell_of(iota((rows8, 128), 1))
-    mid_at = iota((ncy, 128), 0)
-    mid = gauss(mid_at - (CCOL * n + cell_of(iota((ncy, 128), 1))))
-    qf, devf = q_dev((rows8, ncy))
-    outer = jnp.where(qf < CCOL, gauss(CCOL * (devf) + qf - iota((rows8, ncy), 1)), 0.0)
-    cu[:, 256:384] = (-STEP * ADJ_SCALE) * dot(outer, mid, HI)
-    at = CCOL * dev1 + q1 - 2
-    cu[:, 384:512] = jnp.where((at >= 0) & (at < ncy), gauss(at - lane_cell), 0.0)
-    rest = cu[...]
-    for k in range(3):
-        cb[k] = rest.astype(BF16)
-        rest = rest - cb[k].astype(F32)
+    split(ts, 0, gauss(sum_col(256) - (CCOL * n + cell_of(col))))
+    mid = gauss(iota((ncy, 128), 0) - (CCOL * n + cell_of(iota((ncy, 128), 1))))
+    outer = gauss(sum_col(ncy) - iota((nn * 4, ncy), 1))
+    split(ts, 256, (-STEP * ADJ_SCALE) * dot(outer, mid, HI))
+    at = iota((nn * 8, 128), 0)
+    pos = jnp.bitwise_and(at, 63)
+    z, c, x = pos // 8, jnp.bitwise_and(pos // 4, 1), jnp.bitwise_and(pos // 2, 1)
+    at = CCOL * (4 * z + 2 * x + c) + 4 * jnp.bitwise_and(at, 1) + at // 64 - 2
+    lane_cell = CCOL * n + cell_of(iota((nn * 8, 128), 1))
+    split(td, 0, jnp.where((at >= 0) & (at < ncy), gauss(at - lane_cell), 0.0))
 
 
     et0[AIN + 8:, :] = jnp.zeros((EROWS - AIN - 8, 128), F32)
@@ -396,7 +408,7 @@
     ct1[AOUT:, :] = jnp.zeros((CROWS - AOUT, 128), F32)
 
     of_halo(0).wait_recv()
-    assemble(0, own[...])
+    assemble(0, own[0:TX, :])
     ct0[0:AOUT, :] = et0[32:32 + AOUT, :]
     ct1[0:AOUT, :] = et1[32:32 + AOUT, :]
 
@@ -415,16 +427,16 @@
     mask1 = jnp.where(lane < 32, yes(n < nn - 1), yes(n > 0))
 
     def iteration(t, carry):
-        exposure = bl[...] + bk[...]
+        exposure = bl[...] + bk[0:TX, :]
         resist = jax.nn.sigmoid(GAIN * (exposure - LEVEL))
-        own[:, 0:TY] = target_ref[...].astype(F32)
-        error = (resist - own[...]) * GAIN * resist * (1.0 - resist)
+        own[0:TX, 0:TY] = target_ref[...].astype(F32)
+        error = (resist - own[0:TX, :]) * GAIN * resist * (1.0 - resist)
         error = jnp.where(lane < TY, error, 0.0)
-        err[...] = error
+        err[0:TX, :] = error
         half = error.astype(BF16).astype(F32)
-        own[...] = half
+        own[0:TX, :] = half
         field_out(half)
-        resist_ref[...] = resist[:, 0:TY]
+        both_ref[0:TX, :] = resist[:, 0:TY]
 
         start_stage1(0, t, sums_out(col_sum(err)))
         @pl.when(t < ITERS)
@@ -447,7 +459,7 @@
             start_stage2(1, t, rows_result(1, t))
 
         of_halo(t).wait_recv()
-        assemble(t, own[...])
+        assemble(t, own[0:TX, :])
         for k in range(8):
             xa[:, 256 * k:256 * k + 128] = et0[k + 2:k + 2 + AIN, :].astype(BF16)
             xa[:, 256 * k + 128:256 * k + 256] = et1[k + 2:k + 2 + AIN, :].astype(BF16)
@@ -462,22 +474,22 @@
                 at1[...] += piece[lo:lo + AOUT, 128:256]
 
         of_stage2(0, t).wait_recv()
-        turned = turned_back(0, t)
-        out = dot_cols(turned[0:16], 0, 256)
+        turned = turned_sums(t)
+        out = dot_cols(turned[0:16], ts, 0, 256)
         for u in range(COARSE):
             for ref, first in ((ub0, 0), (ub1, 128)):
                 ref[pl.ds(6 + u, 8, stride=COARSE), :] = out[0:8, first:first + 128]
                 ref[pl.ds(206 + u, 8, stride=COARSE), :] = out[8:16, first:first + 128]
         new0 = ct0[0:AOUT, :] - STEP * (at0[...] + ADJ_SCALE * ub0[24:24 + AOUT, :])
         new1 = ct1[0:AOUT, :] - STEP * (at1[...] + ADJ_SCALE * ub1[24:24 + AOUT, :])
-        updated_ref[...] = new0[32:32 + TX, 0:TY]
+        both_ref[TX:, :] = new0[32:32 + TX, 0:TY]
         ct0[0:AOUT, :] = new0.astype(BF16).astype(F32) * (row_ok * mask0)
         ct1[0:AOUT, :] = new1.astype(BF16).astype(F32) * (row_ok * mask1)
 
         @pl.when(t < ITERS)
         def _():
             blur()
-            from_sums = dot_cols(turned[16:24], 256, 384)
+            from_sums = dot_cols(turned[16:24], ts, 256, 384)
             of_stage2(1, t).wait_recv()
             set_back(t, from_sums)
             of_stage1(1, t).wait_send()
@@ -498,24 +510,22 @@
         vmem = pl.BlockSpec(memory_space=pltpu.VMEM)
         f = lambda *shape: pltpu.VMEM(shape, F32)
         h = lambda *shape: pltpu.VMEM(shape, BF16)
-        return pl.pallas_call(
+        both = pl.pallas_call(
             lambda *refs: kernel(ns, nn, *refs),
-            out_shape=(
-                jax.ShapeDtypeStruct((TX, TY), F32),
-                jax.ShapeDtypeStruct((TX, TY), F32),
-            ),
+            out_shape=jax.ShapeDtypeStruct((2 * TX, TY), F32),
             in_specs=[vmem] * 3,
-            out_specs=(vmem, vmem),
+            out_specs=vmem,
             scratch_shapes=[
-                f(2, PHASES, 2 * ns, 8, 128), f(2, PHASES, nn // 2, 4, 128), h(PHASES, HALO, 128),
+                f(PHASES, 2 * ns, 4, 128), f(PHASES, 2 * ns, 8, 128),
+                f(PHASES, nn // 2, 2, 128), f(PHASES, nn // 2, 4, 128), h(PHASES, HALO, 128),
                 h(HALO, 128),
                 f(EROWS, 128), f(EROWS, 128), f(CROWS, 128), f(CROWS, 128),
                 f(AOUT, 128), f(AOUT, 128),
                 h(8, 2048, 256), h(4, 2048, 256), h(80, 3200),
                 f(64, 128), f(64, 128), f(64, 128), f(128, 128),
                 h(AIN, 2048), h(BIN, 2048),
-                f(TX, 128), f(TX, 128), f(40, 128), f(16, 128),
-                h(128, 512), f(nn * 8, 512), h(3, nn * 8, 512), f(416, 128), f(416, 128), f(TX, 128), f(TX, 128),
+                f(232, 128), f(232, 128), f(40, 128), f(16, 128),
+                h(128, 512), h(3, nn * 4, 384), h(3, nn * 8, 128), f(448, 128), f(448, 128), f(232, 128), f(TX, 128),
                 pltpu.SemaphoreType.DMA((5,)), pltpu.SemaphoreType.DMA((PHASES, 5)),
             ],
             compiler_params=pltpu.CompilerParams(
@@ -523,6 +533,7 @@
             ),
             name="dose",
         )(dose, target, psf)
+        return both[0:TX], both[TX:]
 
     return jax.shard_map(
         per_device, mesh=mesh,

time: 73.1 us -> 71.3 us (0.975)
  Pallas kernels: 70.1 us -> 68.9 us
    unnamed x4 -> x0, local copies, waits for them, and re-layouts: 2.22 us -> none
    slice x0 -> x1, local copies, waits for them, and re-layouts: none -> 1.64 us  [per_device(): return (both[0:TX], both[TX:])]
    pallas_call x1, Pallas kernels: 70.1 us -> 68.9 us  [per_device(): pl.pallas_call(lambda *refs: kernel(ns, nn, *refs), out_shape=jax.ShapeDt...]
where the time goes in v3:
time: 71.3 us; the launch traced here: 71.2 us
  Pallas kernels  68.9 us (97%)
  local copies, waits for them, and re-layouts  1.64 us (2%)
    pallas_call x1, Pallas kernels, per_device(): pl.pallas_call(lambda *refs: kernel(ns, nn, *refs), out_shape=jax.ShapeDt...  68.9 us
    slice x1, local copies, waits for them, and re-layouts, per_device(): return (both[0:TX], both[TX:])  1.64 us

profile of v3, /device:TPU:1, one launch (start us, length us, event | category | flops | bytes accessed | tf_op | source)
XLA Modules:
  0.0 71.2 jit_solution(3430077325101964997)
XLA Ops:
  0.6 68.9 %dose.1 = f32[400,100]{1,0:T(8,128)} custom-call(bf16[200,100]{1,0:T(8,128)(2,1)} %refs_0_.1, s32[200,100]{1,0:T(8,128)} %refs_1_.1, bf16[61,61]{1,0:T(8,128)(2,1)} %refs_2_.1), custom_call_target="tpu_custom_call" | custom-call | tf_op jit(solution)/shard_map/dose/pallas_call | solution.py:513
  69.5 1.6 %fusion = (f32[200,100]{1,0:T(8,128)}, f32[200,100]{1,0:T(8,128)}) fusion(f32[400,100]{1,0:T(8,128)} %dose.1), kind=kLoop, calls=%fused_computation | loop fusion | bytes 320000 | tf_op jit(solution)/shard_map/slice | solution.py:536

commit v4 on v3

--- a/solution.py
+++ b/solution.py
@@ -66,10 +66,10 @@
 
 
 def kernel(
-    ns, nn, dose_ref, target_ref, psf_ref, both_ref,
+    ns, nn, dose_hbm, target_hbm, psf_hbm, both_hbm, dose_ref, target_ref, psf_ref, both_ref,
     gs1, gd1, gs2, gd2, halo, tile, et0, et1, ct0, ct1, at0, at1, wa, wf, vv,
     ps, rf, ra, fr, xa, xb, err, own, zs, sc, mw, ts, td, ub0, ub1, bk, bl,
-    send_sem, recv_sem,
+    send_sem, recv_sem, local_sem,
 ):
     s = lax.axis_index("stripe")
     n = lax.axis_index("scan")
@@ -102,6 +102,15 @@
         hello(s, b)
     for a, b in plane + column:
         hello(a, b)
+
+    get_dose = pltpu.make_async_copy(dose_hbm, dose_ref, local_sem.at[0])
+    get_psf = pltpu.make_async_copy(psf_hbm, psf_ref, local_sem.at[1])
+    get_target = pltpu.make_async_copy(target_hbm, target_ref, local_sem.at[2])
+    get_dose.start()
+    get_psf.start()
+    get_target.start()
+    put_resist = pltpu.make_async_copy(both_ref.at[pl.ds(0, TX)], both_hbm.at[pl.ds(0, TX)], local_sem.at[3])
+    put_dose = pltpu.make_async_copy(both_ref.at[pl.ds(TX, TX)], both_hbm.at[pl.ds(TX, TX)], local_sem.at[4])
 
     lane = iota((1, 128), 1)
 
@@ -289,7 +298,16 @@
             blurred = both if blurred is None else blurred + both
         bl[...] = blurred
 
+    get_dose.wait()
+    dose = jnp.zeros((TX, 128), F32)
+    own[0:TX, :] = dose
+    own[0:TX, 0:TY] = dose_ref[...].astype(F32)
+    tile[...] = jnp.zeros_like(tile)
+    field_out(own[0:TX, :])
+    first_payload = cells_out(col_sum(own), None)
+
     ps[...] = jnp.zeros_like(ps)
+    get_psf.wait()
     ps[0:TAPS, 0:TAPS] = psf_ref[...].astype(F32)
     taps = ps[...]
     taps_h = taps.astype(BF16)
@@ -299,13 +317,6 @@
     flip = jnp.where(iota((64, 64), 1) == TAPS - 1 - iota((64, 64), 0), 1.0, 0.0).astype(BF16)
     rf[...] = dot(taps_h, perm_f)
     ra[...] = dot(dot(flip, taps_h).astype(BF16), perm_a)
-
-    dose = jnp.zeros((TX, 128), F32)
-    own[0:TX, :] = dose
-    own[0:TX, 0:TY] = dose_ref[...].astype(F32)
-    tile[...] = jnp.zeros_like(tile)
-    field_out(own[0:TX, :])
-    first_payload = cells_out(col_sum(own), None)
 
     g_row = jnp.bitwise_and(b_at, 63)
     l32 = jnp.bitwise_and(l_at, 31)
@@ -426,6 +437,8 @@
     mask0 = jnp.where(lane < TY, 1.0, yes(n < nn - 1))
     mask1 = jnp.where(lane < 32, yes(n < nn - 1), yes(n > 0))
 
+    get_target.wait()
+
     def iteration(t, carry):
         exposure = bl[...] + bk[0:TX, :]
         resist = jax.nn.sigmoid(GAIN * (exposure - LEVEL))
@@ -437,6 +450,11 @@
         own[0:TX, :] = half
         field_out(half)
         both_ref[0:TX, :] = resist[:, 0:TY]
+
+        @pl.when(t == ITERS)
+        def _():
+            put_resist.start()
+
 
         start_stage1(0, t, sums_out(col_sum(err)))
         @pl.when(t < ITERS)
@@ -501,21 +519,25 @@
         return carry
 
     lax.fori_loop(1, PHASES, iteration, 0)
+    put_dose.start()
+    put_resist.wait()
+    put_dose.wait()
 
 
 def solution(mesh):
     ns, nn = mesh.shape["stripe"], mesh.shape["scan"]
 
     def per_device(dose, target, psf):
-        vmem = pl.BlockSpec(memory_space=pltpu.VMEM)
+        held = pl.BlockSpec(memory_space=pl.ANY)
         f = lambda *shape: pltpu.VMEM(shape, F32)
         h = lambda *shape: pltpu.VMEM(shape, BF16)
         both = pl.pallas_call(
             lambda *refs: kernel(ns, nn, *refs),
             out_shape=jax.ShapeDtypeStruct((2 * TX, TY), F32),
-            in_specs=[vmem] * 3,
-            out_specs=vmem,
+            in_specs=[held] * 3,
+            out_specs=held,
             scratch_shapes=[
+                h(TX, TY), pltpu.VMEM((TX, TY), jnp.int32), h(TAPS, TAPS), f(2 * TX, TY),
                 f(PHASES, 2 * ns, 4, 128), f(PHASES, 2 * ns, 8, 128),
                 f(PHASES, nn // 2, 2, 128), f(PHASES, nn // 2, 4, 128), h(PHASES, HALO, 128),
                 h(HALO, 128),
@@ -527,6 +549,7 @@
                 f(232, 128), f(232, 128), f(40, 128), f(16, 128),
                 h(128, 512), h(3, nn * 4, 384), h(3, nn * 8, 128), f(448, 128), f(448, 128), f(232, 128), f(TX, 128),
                 pltpu.SemaphoreType.DMA((5,)), pltpu.SemaphoreType.DMA((PHASES, 5)),
+                pltpu.SemaphoreType.DMA((5,)),
             ],
             compiler_params=pltpu.CompilerParams(
                 collective_id=0, has_side_effects=True, vmem_limit_bytes=60 << 20

time: 71.3 us -> 70.6 us (level)
  no operation moved by 1% of the time
where the time goes in v4:
time: 70.6 us; the launch traced here: 70.5 us
  Pallas kernels  68.2 us (97%)
  local copies, waits for them, and re-layouts  1.64 us (2%)
    pallas_call x1, Pallas kernels, per_device(): pl.pallas_call(lambda *refs: kernel(ns, nn, *refs), out_shape=jax.ShapeDt...  68.2 us
    slice x1, local copies, waits for them, and re-layouts, per_device(): return (both[0:TX], both[TX:])  1.64 us

profile of v4, /device:TPU:1, one launch (start us, length us, event | category | flops | bytes accessed | tf_op | source)
XLA Modules:
  0.0 70.5 jit_solution(8637707075208767322)
XLA Ops:
  0.6 68.2 %dose.1 = f32[400,100]{1,0:T(8,128)} custom-call(bf16[200,100]{1,0:T(8,128)(2,1)} %refs_0_.1, s32[200,100]{1,0:T(8,128)} %refs_1_.1, bf16[61,61]{1,0:T(8,128)(2,1)} %refs_2_.1), custom_call_target="tpu_custom_call" | custom-call | tf_op jit(solution)/shard_map/dose/pallas_call | solution.py:534
  68.8 1.6 %fusion = (f32[200,100]{1,0:T(8,128)}, f32[200,100]{1,0:T(8,128)}) fusion(f32[400,100]{1,0:T(8,128)} %dose.1), kind=kLoop, calls=%fused_computation | loop fusion | bytes 320000 | tf_op jit(solution)/shard_map/slice | solution.py:559

commit v5 on v4

--- a/solution.py
+++ b/solution.py
@@ -68,7 +68,7 @@
 def kernel(
     ns, nn, dose_hbm, target_hbm, psf_hbm, both_hbm, dose_ref, target_ref, psf_ref, both_ref,
     gs1, gd1, gs2, gd2, halo, tile, et0, et1, ct0, ct1, at0, at1, wa, wf, vv,
-    ps, rf, ra, fr, xa, xb, err, own, zs, sc, mw, ts, td, ub0, ub1, bk, bl,
+    ps, rf, ra, fr, xa, xb, err, own, zs, sc, mw, ts, td, ub0, ub1, bk, bl, mk,
     send_sem, recv_sem, local_sem,
 ):
     s = lax.axis_index("stripe")
@@ -438,25 +438,25 @@
     mask1 = jnp.where(lane < 32, yes(n < nn - 1), yes(n > 0))
 
     get_target.wait()
+    mk[...] = jnp.zeros_like(mk)
+    mk[:, 0:TY] = target_ref[...].astype(F32)
 
     def iteration(t, carry):
         exposure = bl[...] + bk[0:TX, :]
         resist = jax.nn.sigmoid(GAIN * (exposure - LEVEL))
-        own[0:TX, 0:TY] = target_ref[...].astype(F32)
-        error = (resist - own[0:TX, :]) * GAIN * resist * (1.0 - resist)
+        error = (resist - mk[...]) * GAIN * resist * (1.0 - resist)
         error = jnp.where(lane < TY, error, 0.0)
         err[0:TX, :] = error
+        start_stage1(0, t, sums_out(col_sum(err)))
         half = error.astype(BF16).astype(F32)
         own[0:TX, :] = half
         field_out(half)
+        start_halo(t)
         both_ref[0:TX, :] = resist[:, 0:TY]
 
         @pl.when(t == ITERS)
         def _():
             put_resist.start()
-
-
-        start_stage1(0, t, sums_out(col_sum(err)))
         @pl.when(t < ITERS)
         def _():
             cells_in = jnp.concatenate(
@@ -466,7 +466,6 @@
             cur_cols = jnp.where(lane < TY, col_sum(ct0.at[pl.ds(32, TX)]), 0.0)
             start_stage1(1, t, cells_out(cur_cols, spread))
 
-        start_halo(t)
 
         of_stage1(0, t).wait_recv()
         start_stage2(0, t, rows_result(0, t))
@@ -547,7 +546,7 @@
                 f(64, 128), f(64, 128), f(64, 128), f(128, 128),
                 h(AIN, 2048), h(BIN, 2048),
                 f(232, 128), f(232, 128), f(40, 128), f(16, 128),
-                h(128, 512), h(3, nn * 4, 384), h(3, nn * 8, 128), f(448, 128), f(448, 128), f(232, 128), f(TX, 128),
+                h(128, 512), h(3, nn * 4, 384), h(3, nn * 8, 128), f(448, 128), f(448, 128), f(232, 128), f(TX, 128), f(TX, 128),
                 pltpu.SemaphoreType.DMA((5,)), pltpu.SemaphoreType.DMA((PHASES, 5)),
                 pltpu.SemaphoreType.DMA((5,)),
             ],

time: 70.6 us -> 70 us (level)
  no operation moved by 1% of the time
where the time goes in v5:
time: 70 us; the launch traced here: 69.9 us
  Pallas kernels  67.6 us (97%)
  local copies, waits for them, and re-layouts  1.64 us (2%)
    pallas_call x1, Pallas kernels, per_device(): pl.pallas_call(lambda *refs: kernel(ns, nn, *refs), out_shape=jax.ShapeDt...  67.6 us
    slice x1, local copies, waits for them, and re-layouts, per_device(): return (both[0:TX], both[TX:])  1.64 us

profile of v5, /device:TPU:1, one launch (start us, length us, event | category | flops | bytes accessed | tf_op | source)
XLA Modules:
  0.0 69.9 jit_solution(17564581655676736843)
XLA Ops:
  0.6 67.6 %dose.1 = f32[400,100]{1,0:T(8,128)} custom-call(bf16[200,100]{1,0:T(8,128)(2,1)} %refs_0_.1, s32[200,100]{1,0:T(8,128)} %refs_1_.1, bf16[61,61]{1,0:T(8,128)(2,1)} %refs_2_.1), custom_call_target="tpu_custom_call" | custom-call | tf_op jit(solution)/shard_map/dose/pallas_call | solution.py:533
  68.3 1.6 %fusion = (f32[200,100]{1,0:T(8,128)}, f32[200,100]{1,0:T(8,128)}) fusion(f32[400,100]{1,0:T(8,128)} %dose.1), kind=kLoop, calls=%fused_computation | loop fusion | bytes 320000 | tf_op jit(solution)/shard_map/slice | solution.py:558
